TPU v7x, 32 devices: a whole 2x2x4 slice. The times are simulated.
32 devices in a mesh: shard: 2 (over y), ctx: 4 (over x, core), tp: 4 (over z).
Axes of the slice: x: 2, y: 2, z: 4, core: 2. Of those that a mesh axis runs over, the one named last changes fastest.
Arguments:
- tokens: bfloat16 [4, 4096, 768], P('shard', ('ctx', 'tp')), may hold values from -6 to 6
- cotangent: bfloat16 [4, 4096, 768], P('shard', ('ctx', 'tp')), may hold values from -6 to 6
- lengths: int32 [4], P('shard'), may hold values from 1024 to 4096, as said below
- query_weight: bfloat16 [768, 768], P('shard', 'tp'), may hold values from -0.4375 to 0.4375
- query_bias: float32 [768], P('tp'), may hold values from -3 to 3
- key_weight: bfloat16 [768, 768], P('shard', 'tp'), may hold values from -0.21875 to 0.21875
- value_weight: bfloat16 [768, 768], P('shard', 'tp'), may hold values from -0.21875 to 0.21875
- value_bias: float32 [768], P('tp'), may hold values from -3 to 3
- out_weight: bfloat16 [768, 768], P('tp', 'shard'), may hold values from -1.75 to 1.75
- out_bias: float32 [768], replicated, may hold values from -3 to 3
- first_gain: float32 [768], replicated, may hold values from 0.1 to 1.9
- first_shift: float32 [768], replicated, may hold values from -3 to 3
- up_weight: bfloat16 [768, 3072], P('shard', 'tp'), may hold values from -0.21875 to 0.21875
- up_bias: float32 [3072], P('tp'), may hold values from -3 to 3
- down_weight: bfloat16 [3072, 768], P('tp', 'shard'), may hold values from -0.109375 to 0.109375
- down_bias: float32 [768], replicated, may hold values from -3 to 3
- second_gain: float32 [768], replicated, may hold values from 0.1 to 1.9
- second_shift: float32 [768], replicated, may hold values from -3 to 3
Outputs:
- output: bfloat16 [4, 4096, 768], P('shard', ('ctx', 'tp'))
- input_grad: bfloat16 [4, 4096, 768], P('shard', ('ctx', 'tp'))
- query_weight_grad: float32 [768, 768], P('shard', 'tp')
- query_bias_grad: float32 [768], replicated
- key_weight_grad: float32 [768, 768], P('shard', 'tp')
- value_weight_grad: float32 [768, 768], P('shard', 'tp')
- value_bias_grad: float32 [768], replicated
- out_weight_grad: float32 [768, 768], P('tp', 'shard')
- out_bias_grad: float32 [768], replicated
- first_gain_grad: float32 [768], replicated
- first_shift_grad: float32 [768], replicated
- up_weight_grad: float32 [768, 3072], P('shard', 'tp')
- up_bias_grad: float32 [3072], replicated
- down_weight_grad: float32 [3072, 768], P('tp', 'shard')
- down_bias_grad: float32 [768], replicated
- second_gain_grad: float32 [768], replicated
- second_shift_grad: float32 [768], replicated
Inputs may be any that keep to these rules, and one draw needn't show every extreme that they name: `lengths`: positions below a sequence's length are its tokens, the rest padding; some sequence has exactly 4096 valid positions and some exactly 1024.
All inputs are finite; a program needn't handle non-finite values.
Results may differ from a plain program's by a relative error of at most 0.023.
Values may be sent and summed in bfloat16 or wider, within the bound.
No kernel may reach another device: no remote copies, remote signals or barrier semaphores. Data moves between devices by JAX's collectives and lax.ppermute only.
A program may use at most 128 MiB of HBM per device.

v0:
```python
import jax
import jax.numpy as jnp
from jax import lax
from jax.sharding import PartitionSpec as P

HD = 64


epsilon = 1e-12
masked_score = -1e30


def norm_forward(resid, gain, shift):
    centre = resid - jnp.mean(resid, axis=-1, keepdims=True)
    factor = lax.rsqrt(jnp.mean(centre * centre, axis=-1, keepdims=True) + epsilon)
    normed = centre * factor
    return (normed * gain + shift, normed, factor)


def norm_backward(grad_out, normed, factor, gain):
    scaled = grad_out * gain
    centred = scaled - jnp.mean(scaled, axis=-1, keepdims=True)
    return factor * (centred - normed * jnp.mean(scaled * normed, axis=-1, keepdims=True))


def exact_gelu(value):
    return jax.nn.gelu(value, approximate=False)


def key_block(matrix, number, key_size, head_count):
    return lax.dynamic_slice_in_dim(matrix, number * key_size, key_size, 0).reshape(
        key_size, head_count, HD
    )


def block_scores(query_block, keys_here, number, key_size, length):
    scores = jnp.einsum(
        "qhd,khd->hqk", query_block, keys_here, preferred_element_type=jnp.float32
    ) * HD ** (-0.5)
    key_mask = number * key_size + jnp.arange(key_size) < length
    return (scores, key_mask[None, None, :])


def add_rows(matrix, term, first_row):
    before = lax.dynamic_slice_in_dim(matrix, first_row, term.shape[0], 0)
    return lax.dynamic_update_slice_in_dim(matrix, before + term, first_row, 0)


def attend_forward(queries, keys, values, length):
    query_rows, head_width = queries.shape
    head_count = head_width // HD
    key_rows = keys.shape[0]
    query_size = min(512, query_rows)
    key_size = min(512, key_rows // 4)
    key_steps = key_rows // key_size

    def one_block(query_block):

        def first_pass(number, partial_value):
            maximum_now, exp_total = partial_value
            scores, key_mask = block_scores(
                query_block, key_block(keys, number, key_size, head_count), number, key_size, length
            )
            maximum_new = jnp.maximum(
                maximum_now, jnp.max(jnp.where(key_mask, scores, masked_score), axis=-1)
            )
            shifted = jnp.where(key_mask, jnp.exp(scores - maximum_new[..., None]), 0.0)
            return (
                maximum_new,
                exp_total * jnp.exp(maximum_now - maximum_new) + jnp.sum(shifted, axis=-1),
            )

        start_state = (
            jnp.full((head_count, query_size), masked_score, jnp.float32),
            jnp.zeros((head_count, query_size), jnp.float32),
        )
        maximum_now, exp_total = lax.fori_loop(0, key_steps, first_pass, start_state)
        log_totals = maximum_now + jnp.log(exp_total)

        def second_pass(number, summed):
            scores, key_mask = block_scores(
                query_block, key_block(keys, number, key_size, head_count), number, key_size, length
            )
            softmax = jnp.where(key_mask, jnp.exp(scores - log_totals[..., None]), 0.0).astype(
                jnp.bfloat16
            )
            return summed + jnp.einsum(
                "hqk,khd->qhd",
                softmax,
                key_block(values, number, key_size, head_count),
                preferred_element_type=jnp.float32,
            )

        summed = lax.fori_loop(
            0, key_steps, second_pass, jnp.zeros((query_size, head_count, HD), jnp.float32)
        )
        return (summed, log_totals)

    attended, log_totals = lax.map(
        one_block, queries.reshape(query_rows // query_size, query_size, head_count, HD)
    )
    return (attended.reshape(query_rows, head_width), log_totals)


def attend_backward(queries, keys, values, attended, attended_grad, log_totals, length):
    query_rows, head_width = queries.shape
    head_count = head_width // HD
    key_rows = keys.shape[0]
    query_size = min(512, query_rows)
    key_size = min(512, key_rows // 4)
    key_steps = key_rows // key_size

    def to_blocks(matrix):
        return matrix.reshape(query_rows // query_size, query_size, head_count, HD)

    def one_block(key_value, entries):
        query_block, grad_block, out_block, block_totals = entries
        row_dot = jnp.einsum("qhd,qhd->hq", grad_block.astype(jnp.float32), out_block)

        def inner(number, partial_value):
            query_grad, key_grads, value_grads = partial_value
            keys_here = key_block(keys, number, key_size, head_count)
            values_here = key_block(values, number, key_size, head_count)
            scores, key_mask = block_scores(query_block, keys_here, number, key_size, length)
            softmax = jnp.where(key_mask, jnp.exp(scores - block_totals[..., None]), 0.0)
            prob_grad = jnp.einsum(
                "qhd,khd->hqk", grad_block, values_here, preferred_element_type=jnp.float32
            )
            score_grad = (softmax * (prob_grad - row_dot[..., None])).astype(jnp.bfloat16)
            query_grad = query_grad + jnp.einsum(
                "hqk,khd->qhd", score_grad, keys_here, preferred_element_type=jnp.float32
            ) * HD ** (-0.5)
            key_term = jnp.einsum(
                "hqk,qhd->khd", score_grad, query_block, preferred_element_type=jnp.float32
            ) * HD ** (-0.5)
            value_term = jnp.einsum(
                "hqk,qhd->khd",
                softmax.astype(jnp.bfloat16),
                grad_block,
                preferred_element_type=jnp.float32,
            )
            key_grads = add_rows(
                key_grads, key_term.reshape(key_size, head_width), number * key_size
            )
            value_grads = add_rows(
                value_grads, value_term.reshape(key_size, head_width), number * key_size
            )
            return (query_grad, key_grads, value_grads)

        start_state = (
            jnp.zeros((query_size, head_count, HD), jnp.float32),
            key_value[0],
            key_value[1],
        )
        query_grad, key_grads, value_grads = lax.fori_loop(0, key_steps, inner, start_state)
        return ((key_grads, value_grads), query_grad)

    empty_grads = (
        jnp.zeros((key_rows, head_width), jnp.float32),
        jnp.zeros((key_rows, head_width), jnp.float32),
    )
    (key_grads, value_grads), query_grads = lax.scan(
        one_block,
        empty_grads,
        (to_blocks(queries), to_blocks(attended_grad), to_blocks(attended), log_totals),
    )
    return (query_grads.reshape(query_rows, head_width), key_grads, value_grads)


def on_device(
    tokens,
    cotangent,
    lengths,
    query_weight,
    query_bias,
    key_weight,
    value_weight,
    value_bias,
    out_weight,
    out_bias,
    first_gain,
    first_shift,
    up_weight,
    up_bias,
    down_weight,
    down_bias,
    second_gain,
    second_shift,
):
    tp_count = lax.axis_size("tp")
    share_rows = tokens.shape[1]
    block_rows = share_rows * tp_count
    head_width = query_weight.shape[1]
    hidden_width = up_weight.shape[1]
    positions = (
        lax.axis_index("ctx") * block_rows
        + lax.axis_index("tp") * share_rows
        + jnp.arange(share_rows)
    )

    def reduce_grads(matrices):
        pieces = (
            lax.psum_scatter(matrices[0], ("shard", "ctx"), scatter_dimension=0, tiled=True),
            lax.psum_scatter(matrices[1], ("shard", "ctx"), scatter_dimension=0, tiled=True),
            lax.psum_scatter(matrices[2], ("shard", "ctx"), scatter_dimension=0, tiled=True),
            lax.psum_scatter(matrices[3], ("shard", "ctx"), scatter_dimension=1, tiled=True),
            lax.psum_scatter(matrices[4], ("shard", "ctx"), scatter_dimension=0, tiled=True),
            lax.psum_scatter(matrices[5], ("shard", "ctx"), scatter_dimension=1, tiled=True),
        )
        return (
            lax.all_gather(pieces[0].astype(jnp.bfloat16), "ctx", axis=0, tiled=True).astype(
                jnp.float32
            ),
            lax.all_gather(pieces[1].astype(jnp.bfloat16), "ctx", axis=0, tiled=True).astype(
                jnp.float32
            ),
            lax.all_gather(pieces[2].astype(jnp.bfloat16), "ctx", axis=0, tiled=True).astype(
                jnp.float32
            ),
            lax.all_gather(pieces[3].astype(jnp.bfloat16), "ctx", axis=1, tiled=True).astype(
                jnp.float32
            ),
            lax.all_gather(pieces[4].astype(jnp.bfloat16), "ctx", axis=0, tiled=True).astype(
                jnp.float32
            ),
            lax.all_gather(pieces[5].astype(jnp.bfloat16), "ctx", axis=1, tiled=True).astype(
                jnp.float32
            ),
        )

    def micro_batch(gathered, entries):
        query_full, key_full, value_full, out_full, up_full, down_full = gathered
        seq_tokens, seq_cotangent, length = entries
        token_block = lax.all_gather(seq_tokens, "tp", axis=0, tiled=True)
        queries = (
            jnp.dot(token_block, query_full, preferred_element_type=jnp.float32) + query_bias
        ).astype(jnp.bfloat16)
        keys = jnp.dot(token_block, key_full, preferred_element_type=jnp.float32).astype(
            jnp.bfloat16
        )
        values = (
            jnp.dot(token_block, value_full, preferred_element_type=jnp.float32) + value_bias
        ).astype(jnp.bfloat16)
        all_keys, all_values = (
            lax.all_gather(keys, "ctx", axis=0, tiled=True),
            lax.all_gather(values, "ctx", axis=0, tiled=True),
        )
        attended, log_totals = attend_forward(queries, all_keys, all_values, length)
        attended_low = attended.astype(jnp.bfloat16)
        mixed = (
            lax.psum_scatter(
                jnp.dot(attended_low, out_full, preferred_element_type=jnp.float32).astype(
                    jnp.bfloat16
                ),
                "tp",
                scatter_dimension=0,
                tiled=True,
            ).astype(jnp.float32)
            + out_bias
        )
        hidden, first_normed, first_factor = norm_forward(
            seq_tokens.astype(jnp.float32) + mixed, first_gain, first_shift
        )
        hidden_block = lax.all_gather(hidden.astype(jnp.bfloat16), "tp", axis=0, tiled=True)
        pre_act = jnp.dot(hidden_block, up_full, preferred_element_type=jnp.float32) + up_bias
        activated = exact_gelu(pre_act).astype(jnp.bfloat16)
        ffn_out = (
            lax.psum_scatter(
                jnp.dot(activated, down_full, preferred_element_type=jnp.float32).astype(
                    jnp.bfloat16
                ),
                "tp",
                scatter_dimension=0,
                tiled=True,
            ).astype(jnp.float32)
            + down_bias
        )
        result, second_normed, second_factor = norm_forward(
            hidden + ffn_out, second_gain, second_shift
        )
        valid_rows = (positions < length).astype(jnp.float32)[:, None]
        grad_result = seq_cotangent.astype(jnp.float32) * valid_rows
        second_gain_grad = jnp.sum(grad_result * second_normed, axis=0)
        second_shift_grad = jnp.sum(grad_result, axis=0)
        grad_second = norm_backward(grad_result, second_normed, second_factor, second_gain)
        ffn_grad = grad_second.astype(jnp.bfloat16)
        down_bias_grad = jnp.sum(ffn_grad.astype(jnp.float32), axis=0)
        ffn_grad_block = lax.all_gather(ffn_grad, "tp", axis=0, tiled=True)
        down_weight_grad = jnp.einsum(
            "tf,td->fd", activated, ffn_grad_block, preferred_element_type=jnp.float32
        )
        act_grad = jnp.einsum(
            "td,fd->tf", ffn_grad_block, down_full, preferred_element_type=jnp.float32
        )
        unused_value, gelu_pull = jax.vjp(exact_gelu, pre_act)
        pre_grad = gelu_pull(act_grad)[0].astype(jnp.bfloat16)
        up_bias_grad = jnp.sum(pre_grad.astype(jnp.float32), axis=0)
        up_weight_grad = jnp.einsum(
            "td,tf->df", hidden_block, pre_grad, preferred_element_type=jnp.float32
        )
        grad_hidden = grad_second + lax.psum_scatter(
            jnp.einsum("tf,df->td", pre_grad, up_full, preferred_element_type=jnp.float32).astype(
                jnp.bfloat16
            ),
            "tp",
            scatter_dimension=0,
            tiled=True,
        ).astype(jnp.float32)
        first_gain_grad = jnp.sum(grad_hidden * first_normed, axis=0)
        first_shift_grad = jnp.sum(grad_hidden, axis=0)
        grad_first = norm_backward(grad_hidden, first_normed, first_factor, first_gain)
        mixer_grad = grad_first.astype(jnp.bfloat16)
        out_bias_grad = jnp.sum(mixer_grad.astype(jnp.float32), axis=0)
        mixer_grad_block = lax.all_gather(mixer_grad, "tp", axis=0, tiled=True)
        out_weight_grad = jnp.einsum(
            "tc,td->cd", attended_low, mixer_grad_block, preferred_element_type=jnp.float32
        )
        attended_grad = jnp.einsum(
            "td,cd->tc", mixer_grad_block, out_full, preferred_element_type=jnp.float32
        ).astype(jnp.bfloat16)
        query_sum, key_terms, value_terms = attend_backward(
            queries, all_keys, all_values, attended, attended_grad, log_totals, length
        )
        key_sum, value_sum = (
            lax.psum_scatter(
                key_terms.astype(jnp.bfloat16), "ctx", scatter_dimension=0, tiled=True
            ).astype(jnp.float32),
            lax.psum_scatter(
                value_terms.astype(jnp.bfloat16), "ctx", scatter_dimension=0, tiled=True
            ).astype(jnp.float32),
        )
        query_grad = query_sum.astype(jnp.bfloat16)
        key_grad = key_sum.astype(jnp.bfloat16)
        value_grad = value_sum.astype(jnp.bfloat16)
        query_bias_grad = jnp.sum(query_grad.astype(jnp.float32), axis=0)
        value_bias_grad = jnp.sum(value_grad.astype(jnp.float32), axis=0)
        query_weight_grad = jnp.einsum(
            "td,tc->dc", token_block, query_grad, preferred_element_type=jnp.float32
        )
        key_weight_grad = jnp.einsum(
            "td,tc->dc", token_block, key_grad, preferred_element_type=jnp.float32
        )
        value_weight_grad = jnp.einsum(
            "td,tc->dc", token_block, value_grad, preferred_element_type=jnp.float32
        )
        summed = jnp.einsum("tc,dc->td", query_grad, query_full, preferred_element_type=jnp.float32)
        summed = summed + jnp.einsum(
            "tc,dc->td", key_grad, key_full, preferred_element_type=jnp.float32
        )
        input_grad = grad_first + lax.psum_scatter(
            (
                summed
                + jnp.einsum(
                    "tc,dc->td", value_grad, value_full, preferred_element_type=jnp.float32
                )
            ).astype(jnp.bfloat16),
            "tp",
            scatter_dimension=0,
            tiled=True,
        ).astype(jnp.float32)
        matrix_grads = (
            query_weight_grad,
            key_weight_grad,
            value_weight_grad,
            out_weight_grad,
            up_weight_grad,
            down_weight_grad,
        )
        vector_grads = (
            query_bias_grad,
            value_bias_grad,
            out_bias_grad,
            first_gain_grad,
            first_shift_grad,
            up_bias_grad,
            down_bias_grad,
            second_gain_grad,
            second_shift_grad,
        )
        return (
            (result.astype(jnp.bfloat16), input_grad.astype(jnp.bfloat16)),
            matrix_grads,
            vector_grads,
        )

    def micro_step(running, entries):
        gathered = (
            lax.all_gather(query_weight, "shard", axis=0, tiled=True),
            lax.all_gather(key_weight, "shard", axis=0, tiled=True),
            lax.all_gather(value_weight, "shard", axis=0, tiled=True),
            lax.all_gather(out_weight, "shard", axis=1, tiled=True),
            lax.all_gather(up_weight, "shard", axis=0, tiled=True),
            lax.all_gather(down_weight, "shard", axis=1, tiled=True),
        )
        outputs, matrix_grads, vector_grads = micro_batch(gathered, entries)
        matrix_grads = reduce_grads(matrix_grads)
        return (jax.tree.map(jnp.add, running, (matrix_grads, vector_grads)), outputs)

    matrix_start = tuple(
        (
            jnp.zeros(member.shape, jnp.float32)
            for member in (
                query_weight,
                key_weight,
                value_weight,
                out_weight,
                up_weight,
                down_weight,
            )
        )
    )
    model_width = tokens.shape[2]
    vector_start = (
        jnp.zeros((head_width,), jnp.float32),
        jnp.zeros((head_width,), jnp.float32),
        jnp.zeros((model_width,), jnp.float32),
        jnp.zeros((model_width,), jnp.float32),
        jnp.zeros((model_width,), jnp.float32),
        jnp.zeros((hidden_width,), jnp.float32),
        jnp.zeros((model_width,), jnp.float32),
        jnp.zeros((model_width,), jnp.float32),
        jnp.zeros((model_width,), jnp.float32),
    )
    (matrix_sums, vector_sums), (outputs, input_grads) = lax.scan(
        micro_step, (matrix_start, vector_start), (tokens, cotangent, lengths)
    )
    tp_offset = lax.axis_index("tp")

    def spread(vector, full_size):
        return lax.dynamic_update_slice_in_dim(
            jnp.zeros((full_size,), jnp.float32), vector, tp_offset * vector.shape[0], 0
        )

    totals = lax.psum(
        (
            spread(vector_sums[0], head_width * tp_count),
            spread(vector_sums[1], head_width * tp_count),
            vector_sums[2],
            vector_sums[3],
            vector_sums[4],
            spread(vector_sums[5], hidden_width * tp_count),
            vector_sums[6],
            vector_sums[7],
            vector_sums[8],
        ),
        ("shard", "ctx", "tp"),
    )
    return (
        outputs,
        input_grads,
        matrix_sums[0],
        totals[0],
        matrix_sums[1],
        matrix_sums[2],
        totals[1],
        matrix_sums[3],
        totals[2],
        totals[3],
        totals[4],
        matrix_sums[4],
        totals[5],
        matrix_sums[5],
        totals[6],
        totals[7],
        totals[8],
    )


def solution(mesh):
    placed = (
        P("shard", ("ctx", "tp"), None),
        P("shard", ("ctx", "tp"), None),
        P("shard"),
        P("shard", "tp"),
        P("tp"),
        P("shard", "tp"),
        P("shard", "tp"),
        P("tp"),
        P("tp", "shard"),
        P(),
        P(),
        P(),
        P("shard", "tp"),
        P("tp"),
        P("tp", "shard"),
        P(),
        P(),
        P(),
    )
    return jax.shard_map(
        on_device,
        mesh=mesh,
        in_specs=placed,
        out_specs=(
            P("shard", ("ctx", "tp"), None),
            P("shard", ("ctx", "tp"), None),
            P("shard", "tp"),
            P(),
            P("shard", "tp"),
            P("shard", "tp"),
            P(),
            P("tp", "shard"),
            P(),
            P(),
            P(),
            P("shard", "tp"),
            P(),
            P("tp", "shard"),
            P(),
            P(),
            P(),
        ),
        check_vma=False,
    )
```

profile of v0, /device:TPU:0, one launch (start us, length us, event | category | flops | bytes accessed | tf_op | source)
XLA Modules:
  0.0 1993.8 jit_solution(15518845569694610179)
XLA Ops:
  7.4 1926.7 %while.132 = (s32[]{:T(128)}, f32[384,192]{1,0:T(8,128)}, f32[384,192]{1,0:T(8,128)}, f32[384,192]{1,0:T(8,128)}, f32[192,384]{0,1:T(8,128)}, /*index=5*/f32[384...) while((s32[]{:T(128)}, f32[384,192]{1,0:T(8,128)}, ...), condition=%wide.region_42.43_spmd.clone.clone, body=%wide.region_0.42_spmd.clone.sunk.clone | while | flops 11790605312 | bytes 382063616 | solution.py:424
  17.2 32.4 %all-gather.14.cloned.1.call-done = bf16[1,1024,768]{2,1,0:T(8,128)(2,1)} async-done(((bf16[1,256,768]{2,1,0:T(8,128)(2,1)}), bf16[1,1024,768]{2,1,0:T(8,128)(2,1)}) %all-gather.14.cloned.1.call-update) | async-done | bytes 1572880 | tf_op jit(solution)/shard_map/while/body/eval_jaxpr/all_gather | solution.py:234
  92.6 93.9 %while.130 = (s32[]{:T(128)}, f32[2,512,3,64]{1,3,2,0:T(8,128)S(1)}, f32[2,3,512]{2,1,0:T(4,128)S(1)}, bf16[2,512,3,64]{1,3,2,0:T(8,128)(2,1)S(1)}, s32[]{:T(128...) while((s32[]{:T(128)}, f32[2,512,3,64]{1,3,2,0:T(8,128)S(1)}, ...), condition=%wide.region_8.8_spmd, body=%wide.region_1.7_spmd.sunk | while | flops 310848512 | bytes 10542164 | solution.py:99
  92.6 24.8 %while.133 = (s32[]{:T(128)}, f32[3,512]{1,0:T(4,128)S(1)}, f32[3,512]{1,0:T(4,128)S(1)}, s32[]{:T(128)}, bf16[4096,192]{0,1:T(8,128)(2,1)}, /*index=5*/bf16[512,3,64]{0,2,1:T(8,128)(2,1)S(1)}) while((s32[]{:T(128)}, f32[3,512]{1,0:T(4,128)S(1)}, f32[3,512]{1,0:T(4,128)S(1)}, s32[]{:T(128)}, ...), condition=%wide.region_5.4_spmd.clone.clone, body=%wide.region_2.3_spmd.clone.sunk.clone | while | flops 106177032 | bytes 7159442 | solution.py:77
  117.4 22.1 %while.134 = (s32[]{:T(128)}, f32[512,3,64]{0,2,1:T(8,128)S(1)}, bf16[4096,192]{0,1:T(8,128)(2,1)}, s32[]{:T(128)}, bf16[4096,192]{0,1:T(8,128)(2,1)}, /*index=5*/bf16[512,3,64]{0,2,1:T(8,128)(2,1)S(1)}, f32[3,512]{1,0:T(4,128)S(1)}) while((s32[]{:T(128)}, f32[512,3,64]{0,2,1:T(8,128)S(1)}, ...), condition=%wide.region_7.6_spmd.clone.clone, body=%wide.region_6.5_spmd.clone.sunk.clone | while | flops 204669952 | bytes 2170009 | solution.py:94
  139.6 24.8 %while.133 = (s32[]{:T(128)}, f32[3,512]{1,0:T(4,128)S(1)}, f32[3,512]{1,0:T(4,128)S(1)}, s32[]{:T(128)}, bf16[4096,192]{0,1:T(8,128)(2,1)}, /*index=5*/bf16[512,3,64]{0,2,1:T(8,128)(2,1)S(1)}) while((s32[]{:T(128)}, f32[3,512]{1,0:T(4,128)S(1)}, f32[3,512]{1,0:T(4,128)S(1)}, s32[]{:T(128)}, ...), condition=%wide.region_5.4_spmd.clone.clone, body=%wide.region_2.3_spmd.clone.sunk.clone | while | flops 106177032 | bytes 7159442 | solution.py:77
  164.4 22.1 %while.134 = (s32[]{:T(128)}, f32[512,3,64]{0,2,1:T(8,128)S(1)}, bf16[4096,192]{0,1:T(8,128)(2,1)}, s32[]{:T(128)}, bf16[4096,192]{0,1:T(8,128)(2,1)}, /*index=5*/bf16[512,3,64]{0,2,1:T(8,128)(2,1)S(1)}, f32[3,512]{1,0:T(4,128)S(1)}) while((s32[]{:T(128)}, f32[512,3,64]{0,2,1:T(8,128)S(1)}, ...), condition=%wide.region_7.6_spmd.clone.clone, body=%wide.region_6.5_spmd.clone.sunk.clone | while | flops 204669952 | bytes 2170009 | solution.py:94
  190.7 34.8 %reduce-scatter.18.cloned.1.call-done = bf16[256,768]{1,0:T(8,128)(2,1)} async-done(((bf16[1024,768]{1,0:T(8,128)(2,1)}), bf16[256,768]{1,0:T(8,128)(2,1)}) %reduce-scatter.18.cloned.1.call-update) | async-done | bytes 393232 | tf_op jit(solution)/shard_map/while/body/eval_jaxpr/reduce_scatter | solution.py:251
  248.7 38.6 %all-gather.20.cloned.1.call-done = bf16[1024,768]{1,0:T(8,128)(2,1)} async-done(((bf16[256,768]{1,0:T(8,128)(2,1)}), bf16[1024,768]{1,0:T(8,128)(2,1)}) %all-gather.20.cloned.1.call-update) | async-done | bytes 1572880 | tf_op jit(solution)/shard_map/while/body/eval_jaxpr/all_gather | solution.py:264
  315.6 34.7 %reduce-scatter.20.cloned.1.call-done = bf16[256,768]{1,0:T(8,128)(2,1)} async-done(((bf16[1024,768]{1,0:T(8,128)(2,1)}), bf16[256,768]{1,0:T(8,128)(2,1)}) %reduce-scatter.20.cloned.1.call-update) | async-done | bytes 393232 | tf_op jit(solution)/shard_map/while/body/eval_jaxpr/reduce_scatter | solution.py:268
  354.8 36.2 %all-gather.26.cloned.1.call-done = bf16[1024,768]{1,0:T(8,128)(2,1)} async-done(((bf16[256,768]{1,0:T(8,128)(2,1)}), bf16[1024,768]{1,0:T(8,128)(2,1)}) %all-gather.26.cloned.1.call-update) | async-done | bytes 1572880 | tf_op jit(solution)/shard_map/while/body/eval_jaxpr/all_gather | solution.py:288
  401.4 34.3 %reduce-scatter.22.cloned.1.call-done = bf16[256,768]{1,0:T(8,128)(2,1)} async-done(((bf16[1024,768]{1,0:T(8,128)(2,1)}), bf16[256,768]{1,0:T(8,128)(2,1)}) %reduce-scatter.22.cloned.1.call-update) | async-done | bytes 393232 | tf_op jit(solution)/shard_map/while/body/eval_jaxpr/reduce_scatter | solution.py:301
  441.6 35.4 %all-gather.28.cloned.1.call-done = bf16[1024,768]{1,0:T(8,128)(2,1)} async-done(((bf16[256,768]{1,0:T(8,128)(2,1)}), bf16[1024,768]{1,0:T(8,128)(2,1)}) %all-gather.28.cloned.1.call-update) | async-done | bytes 1572880 | tf_op jit(solution)/shard_map/while/body/eval_jaxpr/all_gather | solution.py:314
  484.2 141.8 %while.131 = (s32[]{:T(128)}, f32[4096,192]{0,1:T(8,128)}, f32[4096,192]{0,1:T(8,128)}, bf16[2,512,3,64]{1,3,2,0:T(8,128)(2,1)}, bf16[2,512,3,64]{1,3,2,0:T(8,12...) while((s32[]{:T(128)}, f32[4096,192]{0,1:T(8,128)}, ...), condition=%wide.region_23.23_spmd, body=%wide.region_20.22_spmd.sunk | while | flops 512065024 | bytes 35637344 | solution.py:162
  488.3 66.0 %while.135 = (s32[]{:T(128)}, f32[512,3,64]{0,2,1:T(8,128)S(1)}, f32[4096,192]{0,1:T(8,128)}, f32[4096,192]{0,1:T(8,128)}, bf16[4096,192]{0,1:T(8,128)(2,1)}, /*...) while((s32[]{:T(128)}, f32[512,3,64]{0,2,1:T(8,128)S(1)}, ...), condition=%wide.region_22.21_spmd.clone.clone, body=%wide.region_21.20_spmd.clone.sunk.clone | while | flops 511771648 | bytes 21057244 | solution.py:155
  559.1 66.0 %while.135 = (s32[]{:T(128)}, f32[512,3,64]{0,2,1:T(8,128)S(1)}, f32[4096,192]{0,1:T(8,128)}, f32[4096,192]{0,1:T(8,128)}, bf16[4096,192]{0,1:T(8,128)(2,1)}, /*...) while((s32[]{:T(128)}, f32[512,3,64]{0,2,1:T(8,128)S(1)}, ...), condition=%wide.region_22.21_spmd.clone.clone, body=%wide.region_21.20_spmd.clone.sunk.clone | while | flops 511771648 | bytes 21057244 | solution.py:155
  659.2 28.1 %reduce-scatter.30.cloned.1.call-done = bf16[1024,192]{0,1:T(8,128)(2,1)} async-done(((bf16[4096,192]{0,1:T(8,128)(2,1)}), bf16[1024,192]{0,1:T(8,128)(2,1)}) %reduce-scatter.30.cloned.1.call-update) | async-done | bytes 393232 | tf_op jit(solution)/shard_map/while/body/eval_jaxpr/reduce_scatter | solution.py:328
  694.3 39.2 %reduce-scatter.38.cloned.1.call-done = f32[768,96]{0,1:T(8,128)} async-done(((f32[768,768]{0,1:T(8,128)}), f32[768,96]{0,1:T(8,128)}) %reduce-scatter.38.cloned.1.call-update) | async-done | bytes 294928 | tf_op jit(solution)/shard_map/while/body/eval_jaxpr/reduce_scatter | solution.py:208
  734.5 44.7 %reduce-scatter.36.cloned.1.call-done = f32[96,768]{1,0:T(8,128)} async-done(((f32[768,768]{1,0:T(8,128)}), f32[96,768]{1,0:T(8,128)}) %reduce-scatter.36.cloned.1.call-update) | async-done | bytes 294928 | tf_op jit(solution)/shard_map/while/body/eval_jaxpr/reduce_scatter | solution.py:207
  797.9 19.4 reduce-scatter.34.cloned.1.call-done
  818.4 36.9 %reduce-scatter.24.cloned.1.call-done = f32[96,192]{1,0:T(8,128)} async-done(((f32[768,192]{1,0:T(8,128)}), f32[96,192]{1,0:T(8,128)}) %reduce-scatter.24.cloned.1.call-update) | async-done | bytes 73744 | tf_op jit(solution)/shard_map/while/body/eval_jaxpr/reduce_scatter | solution.py:203
  867.8 25.9 %reduce-scatter.28.cloned.1.call-done = f32[96,192]{1,0:T(8,128)} async-done(((f32[768,192]{1,0:T(8,128)}), f32[96,192]{1,0:T(8,128)}) %reduce-scatter.28.cloned.1.call-update) | async-done | bytes 73744 | tf_op jit(solution)/shard_map/while/body/eval_jaxpr/reduce_scatter | solution.py:204
  894.5 37.2 %reduce-scatter.32.cloned.1.call-done = f32[96,192]{1,0:T(8,128)} async-done(((f32[768,192]{1,0:T(8,128)}), f32[96,192]{1,0:T(8,128)}) %reduce-scatter.32.cloned.1.call-update) | async-done | bytes 73744 | tf_op jit(solution)/shard_map/while/body/eval_jaxpr/reduce_scatter | solution.py:205
  944.1 25.1 %reduce-scatter.40.cloned.1.call-done = bf16[256,768]{1,0:T(8,128)(2,1)} async-done(((bf16[1024,768]{1,0:T(8,128)(2,1)}), bf16[256,768]{1,0:T(8,128)(2,1)}) %reduce-scatter.40.cloned.1.call-update) | async-done | bytes 393232 | tf_op jit(solution)/shard_map/while/body/eval_jaxpr/reduce_scatter | solution.py:350
  979.5 30.1 %all-gather.14.cloned.1.call-done = bf16[1,1024,768]{2,1,0:T(8,128)(2,1)} async-done(((bf16[1,256,768]{2,1,0:T(8,128)(2,1)}), bf16[1,1024,768]{2,1,0:T(8,128)(2,1)}) %all-gather.14.cloned.1.call-update) | async-done | bytes 1572880 | tf_op jit(solution)/shard_map/while/body/eval_jaxpr/all_gather | solution.py:234
  1052.6 93.9 %while.130 = (s32[]{:T(128)}, f32[2,512,3,64]{1,3,2,0:T(8,128)S(1)}, f32[2,3,512]{2,1,0:T(4,128)S(1)}, bf16[2,512,3,64]{1,3,2,0:T(8,128)(2,1)S(1)}, s32[]{:T(128...) while((s32[]{:T(128)}, f32[2,512,3,64]{1,3,2,0:T(8,128)S(1)}, ...), condition=%wide.region_8.8_spmd, body=%wide.region_1.7_spmd.sunk | while | flops 310848512 | bytes 10542164 | solution.py:99
  1052.6 24.8 %while.133 = (s32[]{:T(128)}, f32[3,512]{1,0:T(4,128)S(1)}, f32[3,512]{1,0:T(4,128)S(1)}, s32[]{:T(128)}, bf16[4096,192]{0,1:T(8,128)(2,1)}, /*index=5*/bf16[512,3,64]{0,2,1:T(8,128)(2,1)S(1)}) while((s32[]{:T(128)}, f32[3,512]{1,0:T(4,128)S(1)}, f32[3,512]{1,0:T(4,128)S(1)}, s32[]{:T(128)}, ...), condition=%wide.region_5.4_spmd.clone.clone, body=%wide.region_2.3_spmd.clone.sunk.clone | while | flops 106177032 | bytes 7159442 | solution.py:77
  1077.4 22.1 %while.134 = (s32[]{:T(128)}, f32[512,3,64]{0,2,1:T(8,128)S(1)}, bf16[4096,192]{0,1:T(8,128)(2,1)}, s32[]{:T(128)}, bf16[4096,192]{0,1:T(8,128)(2,1)}, /*index=5*/bf16[512,3,64]{0,2,1:T(8,128)(2,1)S(1)}, f32[3,512]{1,0:T(4,128)S(1)}) while((s32[]{:T(128)}, f32[512,3,64]{0,2,1:T(8,128)S(1)}, ...), condition=%wide.region_7.6_spmd.clone.clone, body=%wide.region_6.5_spmd.clone.sunk.clone | while | flops 204669952 | bytes 2170009 | solution.py:94
  1099.6 24.8 %while.133 = (s32[]{:T(128)}, f32[3,512]{1,0:T(4,128)S(1)}, f32[3,512]{1,0:T(4,128)S(1)}, s32[]{:T(128)}, bf16[4096,192]{0,1:T(8,128)(2,1)}, /*index=5*/bf16[512,3,64]{0,2,1:T(8,128)(2,1)S(1)}) while((s32[]{:T(128)}, f32[3,512]{1,0:T(4,128)S(1)}, f32[3,512]{1,0:T(4,128)S(1)}, s32[]{:T(128)}, ...), condition=%wide.region_5.4_spmd.clone.clone, body=%wide.region_2.3_spmd.clone.sunk.clone | while | flops 106177032 | bytes 7159442 | solution.py:77
  1124.4 22.1 %while.134 = (s32[]{:T(128)}, f32[512,3,64]{0,2,1:T(8,128)S(1)}, bf16[4096,192]{0,1:T(8,128)(2,1)}, s32[]{:T(128)}, bf16[4096,192]{0,1:T(8,128)(2,1)}, /*index=5*/bf16[512,3,64]{0,2,1:T(8,128)(2,1)S(1)}, f32[3,512]{1,0:T(4,128)S(1)}) while((s32[]{:T(128)}, f32[512,3,64]{0,2,1:T(8,128)S(1)}, ...), condition=%wide.region_7.6_spmd.clone.clone, body=%wide.region_6.5_spmd.clone.sunk.clone | while | flops 204669952 | bytes 2170009 | solution.py:94
  1150.9 34.6 %reduce-scatter.18.cloned.1.call-done = bf16[256,768]{1,0:T(8,128)(2,1)} async-done(((bf16[1024,768]{1,0:T(8,128)(2,1)}), bf16[256,768]{1,0:T(8,128)(2,1)}) %reduce-scatter.18.cloned.1.call-update) | async-done | bytes 393232 | tf_op jit(solution)/shard_map/while/body/eval_jaxpr/reduce_scatter | solution.py:251
  1190.7 18.2 all-gather.22.cloned.1.call-done
  1208.9 38.5 %all-gather.20.cloned.1.call-done = bf16[1024,768]{1,0:T(8,128)(2,1)} async-done(((bf16[256,768]{1,0:T(8,128)(2,1)}), bf16[1024,768]{1,0:T(8,128)(2,1)}) %all-gather.20.cloned.1.call-update) | async-done | bytes 1572880 | tf_op jit(solution)/shard_map/while/body/eval_jaxpr/all_gather | solution.py:264
  1275.6 34.7 %reduce-scatter.20.cloned.1.call-done = bf16[256,768]{1,0:T(8,128)(2,1)} async-done(((bf16[1024,768]{1,0:T(8,128)(2,1)}), bf16[256,768]{1,0:T(8,128)(2,1)}) %reduce-scatter.20.cloned.1.call-update) | async-done | bytes 393232 | tf_op jit(solution)/shard_map/while/body/eval_jaxpr/reduce_scatter | solution.py:268
  1314.9 36.2 %all-gather.26.cloned.1.call-done = bf16[1024,768]{1,0:T(8,128)(2,1)} async-done(((bf16[256,768]{1,0:T(8,128)(2,1)}), bf16[1024,768]{1,0:T(8,128)(2,1)}) %all-gather.26.cloned.1.call-update) | async-done | bytes 1572880 | tf_op jit(solution)/shard_map/while/body/eval_jaxpr/all_gather | solution.py:288
  1361.4 34.2 %reduce-scatter.22.cloned.1.call-done = bf16[256,768]{1,0:T(8,128)(2,1)} async-done(((bf16[1024,768]{1,0:T(8,128)(2,1)}), bf16[256,768]{1,0:T(8,128)(2,1)}) %reduce-scatter.22.cloned.1.call-update) | async-done | bytes 393232 | tf_op jit(solution)/shard_map/while/body/eval_jaxpr/reduce_scatter | solution.py:301
  1401.6 35.4 %all-gather.28.cloned.1.call-done = bf16[1024,768]{1,0:T(8,128)(2,1)} async-done(((bf16[256,768]{1,0:T(8,128)(2,1)}), bf16[1024,768]{1,0:T(8,128)(2,1)}) %all-gather.28.cloned.1.call-update) | async-done | bytes 1572880 | tf_op jit(solution)/shard_map/while/body/eval_jaxpr/all_gather | solution.py:314
  1444.2 141.8 %while.131 = (s32[]{:T(128)}, f32[4096,192]{0,1:T(8,128)}, f32[4096,192]{0,1:T(8,128)}, bf16[2,512,3,64]{1,3,2,0:T(8,128)(2,1)}, bf16[2,512,3,64]{1,3,2,0:T(8,12...) while((s32[]{:T(128)}, f32[4096,192]{0,1:T(8,128)}, ...), condition=%wide.region_23.23_spmd, body=%wide.region_20.22_spmd.sunk | while | flops 512065024 | bytes 35637344 | solution.py:162
  1448.3 66.0 %while.135 = (s32[]{:T(128)}, f32[512,3,64]{0,2,1:T(8,128)S(1)}, f32[4096,192]{0,1:T(8,128)}, f32[4096,192]{0,1:T(8,128)}, bf16[4096,192]{0,1:T(8,128)(2,1)}, /*...) while((s32[]{:T(128)}, f32[512,3,64]{0,2,1:T(8,128)S(1)}, ...), condition=%wide.region_22.21_spmd.clone.clone, body=%wide.region_21.20_spmd.clone.sunk.clone | while | flops 511771648 | bytes 21057244 | solution.py:155
  1519.2 66.0 %while.135 = (s32[]{:T(128)}, f32[512,3,64]{0,2,1:T(8,128)S(1)}, f32[4096,192]{0,1:T(8,128)}, f32[4096,192]{0,1:T(8,128)}, bf16[4096,192]{0,1:T(8,128)(2,1)}, /*...) while((s32[]{:T(128)}, f32[512,3,64]{0,2,1:T(8,128)S(1)}, ...), condition=%wide.region_22.21_spmd.clone.clone, body=%wide.region_21.20_spmd.clone.sunk.clone | while | flops 511771648 | bytes 21057244 | solution.py:155
  1619.3 28.0 %reduce-scatter.30.cloned.1.call-done = bf16[1024,192]{0,1:T(8,128)(2,1)} async-done(((bf16[4096,192]{0,1:T(8,128)(2,1)}), bf16[1024,192]{0,1:T(8,128)(2,1)}) %reduce-scatter.30.cloned.1.call-update) | async-done | bytes 393232 | tf_op jit(solution)/shard_map/while/body/eval_jaxpr/reduce_scatter | solution.py:328
  1654.3 39.3 %reduce-scatter.38.cloned.1.call-done = f32[768,96]{0,1:T(8,128)} async-done(((f32[768,768]{0,1:T(8,128)}), f32[768,96]{0,1:T(8,128)}) %reduce-scatter.38.cloned.1.call-update) | async-done | bytes 294928 | tf_op jit(solution)/shard_map/while/body/eval_jaxpr/reduce_scatter | solution.py:208
  1694.6 44.9 %reduce-scatter.36.cloned.1.call-done = f32[96,768]{1,0:T(8,128)} async-done(((f32[768,768]{1,0:T(8,128)}), f32[96,768]{1,0:T(8,128)}) %reduce-scatter.36.cloned.1.call-update) | async-done | bytes 294928 | tf_op jit(solution)/shard_map/while/body/eval_jaxpr/reduce_scatter | solution.py:207
  1778.6 36.9 %reduce-scatter.24.cloned.1.call-done = f32[96,192]{1,0:T(8,128)} async-done(((f32[768,192]{1,0:T(8,128)}), f32[96,192]{1,0:T(8,128)}) %reduce-scatter.24.cloned.1.call-update) | async-done | bytes 73744 | tf_op jit(solution)/shard_map/while/body/eval_jaxpr/reduce_scatter | solution.py:203
  1828.0 26.0 %reduce-scatter.28.cloned.1.call-done = f32[96,192]{1,0:T(8,128)} async-done(((f32[768,192]{1,0:T(8,128)}), f32[96,192]{1,0:T(8,128)}) %reduce-scatter.28.cloned.1.call-update) | async-done | bytes 73744 | tf_op jit(solution)/shard_map/while/body/eval_jaxpr/reduce_scatter | solution.py:204
  1854.8 37.1 %reduce-scatter.32.cloned.1.call-done = f32[96,192]{1,0:T(8,128)} async-done(((f32[768,192]{1,0:T(8,128)}), f32[96,192]{1,0:T(8,128)}) %reduce-scatter.32.cloned.1.call-update) | async-done | bytes 73744 | tf_op jit(solution)/shard_map/while/body/eval_jaxpr/reduce_scatter | solution.py:205
  1904.3 25.3 %reduce-scatter.40.cloned.1.call-done = bf16[256,768]{1,0:T(8,128)(2,1)} async-done(((bf16[1024,768]{1,0:T(8,128)(2,1)}), bf16[256,768]{1,0:T(8,128)(2,1)}) %reduce-scatter.40.cloned.1.call-update) | async-done | bytes 393232 | tf_op jit(solution)/shard_map/while/body/eval_jaxpr/reduce_scatter | solution.py:350
  1936.7 41.0 %all-reduce = (f32[768]{0:T(1024)}, f32[768]{0:T(1024)}, f32[768]{0:T(1024)}, f32[768]{0:T(1024)}, f32[768]{0:T(1024)}, /*index=5*/f32[3072]{0:T(1024)}, f32[768]{0:T(1024)}, f32[768]{0:T(1024)}, f32[768]{0:T(1024)}) all-reduce(f32[768]{0:T(1024)S(1)} %dynamic_update_slice.41, ...), channel_id=1, replica_groups=mesh['shard'=2,'ctx'=4,'tp'=4] {'shard','ctx','tp'}, use_global_device_ids=true, to_apply=%region_43.44 | all-reduce | flops 9216 | bytes 73728 | tf_op jit(solution)/shard_map/psum | solution.py:434
  (1356 shorter events, 925.6 us)
Async XLA Ops:
  7.4 42.2 %all-gather.14.cloned.1.call-start = ((), (), s32[]{:S(2)}) async-start(), calls=%async_computation.12 | async-start | bytes 1966080 | tf_op jit(solution)/shard_map/while/body/eval_jaxpr/all_gather | solution.py:234
  9.3 65.2 %all-gather.18.cloned.1.call-start = ((), (), s32[]{:S(2)}) async-start(), calls=%async_computation.14 | async-start | bytes 1966080 | tf_op jit(solution)/shard_map/while/body/eval_jaxpr/all_gather | solution.py:246
  52.6 39.9 %all-gather.16.cloned.1.call-start = ((), (), s32[]{:S(2)}) async-start(), calls=%async_computation.13 | async-start | bytes 1966080 | tf_op jit(solution)/shard_map/while/body/eval_jaxpr/all_gather | solution.py:245
  61.0 164.4 %reduce-scatter.18.cloned.1.call-start = ((), (), s32[]{:S(2)}) async-start(), calls=%async_computation.15 | async-start | bytes 1966080 | tf_op jit(solution)/shard_map/while/body/eval_jaxpr/reduce_scatter | solution.py:251
  190.0 58.6 %all-gather.22.cloned.1.call-start = ((), (), s32[]{:S(2)}) async-start(), calls=%async_computation.17 | async-start | bytes 1769472 | tf_op jit(solution)/shard_map/while/body/eval_jaxpr/all_gather | solution.py:392
  190.6 96.6 %all-gather.20.cloned.1.call-start = ((), (), s32[]{:S(2)}) async-start(), calls=%async_computation.16 | async-start | bytes 1966080 | tf_op jit(solution)/shard_map/while/body/eval_jaxpr/all_gather | solution.py:264
  230.0 80.4 %all-gather.24.cloned.1.call-start = ((), (), s32[]{:S(2)}) async-start(), calls=%async_computation.18 | async-start | bytes 1769472 | tf_op jit(solution)/shard_map/while/body/eval_jaxpr/all_gather | solution.py:393
  230.7 119.5 %reduce-scatter.20.cloned.1.call-start = ((), (), s32[]{:S(2)}) async-start(), calls=%async_computation.19 | async-start | bytes 1966080 | tf_op jit(solution)/shard_map/while/body/eval_jaxpr/reduce_scatter | solution.py:268
  314.8 76.2 %all-gather.26.cloned.1.call-start = ((), (), s32[]{:S(2)}) async-start(), calls=%async_computation.20 | async-start | bytes 1966080 | tf_op jit(solution)/shard_map/while/body/eval_jaxpr/all_gather | solution.py:288
  354.8 80.8 %reduce-scatter.22.cloned.1.call-start = ((), (), s32[]{:S(2)}) async-start(), calls=%async_computation.21 | async-start | bytes 1966080 | tf_op jit(solution)/shard_map/while/body/eval_jaxpr/reduce_scatter | solution.py:301
  401.3 75.7 %all-gather.28.cloned.1.call-start = ((), (), s32[]{:S(2)}) async-start(), calls=%async_computation.22 | async-start | bytes 1966080 | tf_op jit(solution)/shard_map/while/body/eval_jaxpr/all_gather | solution.py:314
  440.8 215.7 %reduce-scatter.26.cloned.1.call-start = ((), (), s32[]{:S(2)}) async-start(), calls=%async_computation.24 | async-start | bytes 1966080 | tf_op jit(solution)/shard_map/while/body/eval_jaxpr/reduce_scatter | solution.py:325
  629.3 58.1 %reduce-scatter.30.cloned.1.call-start = ((), (), s32[]{:S(2)}) async-start(), calls=%async_computation.26 | async-start | bytes 1966080 | tf_op jit(solution)/shard_map/while/body/eval_jaxpr/reduce_scatter | solution.py:328
  630.8 102.7 %reduce-scatter.38.cloned.1.call-start = ((), (), s32[]{:S(2)}) async-start(), calls=%async_computation.30 | async-start | bytes 2654208 | tf_op jit(solution)/shard_map/while/body/eval_jaxpr/reduce_scatter | solution.py:208
  635.8 143.4 %reduce-scatter.36.cloned.1.call-start = ((), (), s32[]{:S(2)}) async-start(), calls=%async_computation.29 | async-start | bytes 2654208 | tf_op jit(solution)/shard_map/while/body/eval_jaxpr/reduce_scatter | solution.py:207
  638.8 178.4 %reduce-scatter.34.cloned.1.call-start = ((), (), s32[]{:S(2)}) async-start(), calls=%async_computation.28 | async-start | bytes 884736 | tf_op jit(solution)/shard_map/while
  642.2 213.1 %reduce-scatter.24.cloned.1.call-start = ((), (), s32[]{:S(2)}) async-start(), calls=%async_computation.23 | async-start | bytes 884736 | tf_op jit(solution)/shard_map/while/body/eval_jaxpr/reduce_scatter | solution.py:203
  644.3 249.3 %reduce-scatter.28.cloned.1.call-start = ((), (), s32[]{:S(2)}) async-start(), calls=%async_computation.25 | async-start | bytes 884736 | tf_op jit(solution)/shard_map/while/body/eval_jaxpr/reduce_scatter | solution.py:204
  659.0 272.8 %reduce-scatter.32.cloned.1.call-start = ((), (), s32[]{:S(2)}) async-start(), calls=%async_computation.27 | async-start | bytes 884736 | tf_op jit(solution)/shard_map/while/body/eval_jaxpr/reduce_scatter | solution.py:205
  690.0 279.2 %reduce-scatter.40.cloned.1.call-start = ((), (), s32[]{:S(2)}) async-start(), calls=%async_computation.31 | async-start | bytes 1966080 | tf_op jit(solution)/shard_map/while/body/eval_jaxpr/reduce_scatter | solution.py:350
  796.5 147.4 %copy-start.30 = (f32[384,192]{1,0:T(8,128)S(1)}, f32[384,192]{1,0:T(8,128)}, u32[]{:S(2)}) copy-start(f32[384,192]{1,0:T(8,128)} %get-tuple-element.2370) | copy-start | bytes 884740 | tf_op jit(solution)/shard_map/while
  797.6 146.4 %copy-start.28 = (f32[384,192]{1,0:T(8,128)S(1)}, f32[384,192]{1,0:T(8,128)}, u32[]{:S(2)}) copy-start(f32[384,192]{1,0:T(8,128)} %get-tuple-element.2371) | copy-start | bytes 884740 | tf_op jit(solution)/shard_map/while
  797.6 171.6 %copy-start.16 = (f32[256,768]{1,0:T(8,128)S(1)}, f32[256,768]{1,0:T(8,128)}, u32[]{:S(2)}) copy-start(f32[256,768]{1,0:T(8,128)} %get-tuple-element.2017) | copy-start | bytes 2359300 | tf_op jit(solution)/shard_map/while
  797.9 173.2 %copy-start.72 = (f32[192]{0:T(256)}, f32[192]{0:T(256)S(1)}, u32[]{:S(2)}) copy-start(f32[192]{0:T(256)S(1)} %select_add_fusion.47) | copy-start | bytes 2308 | tf_op jit(solution)/shard_map/while
  971.1 38.5 %all-gather.14.cloned.1.call-start = ((), (), s32[]{:S(2)}) async-start(), calls=%async_computation.12 | async-start | bytes 1966080 | tf_op jit(solution)/shard_map/while/body/eval_jaxpr/all_gather | solution.py:234
  973.0 61.5 %all-gather.18.cloned.1.call-start = ((), (), s32[]{:S(2)}) async-start(), calls=%async_computation.14 | async-start | bytes 1966080 | tf_op jit(solution)/shard_map/while/body/eval_jaxpr/all_gather | solution.py:246
  1012.7 39.9 %all-gather.16.cloned.1.call-start = ((), (), s32[]{:S(2)}) async-start(), calls=%async_computation.13 | async-start | bytes 1966080 | tf_op jit(solution)/shard_map/while/body/eval_jaxpr/all_gather | solution.py:245
  1021.1 164.5 %reduce-scatter.18.cloned.1.call-start = ((), (), s32[]{:S(2)}) async-start(), calls=%async_computation.15 | async-start | bytes 1966080 | tf_op jit(solution)/shard_map/while/body/eval_jaxpr/reduce_scatter | solution.py:251
  1150.1 58.8 %all-gather.22.cloned.1.call-start = ((), (), s32[]{:S(2)}) async-start(), calls=%async_computation.17 | async-start | bytes 1769472 | tf_op jit(solution)/shard_map/while/body/eval_jaxpr/all_gather | solution.py:392
  1150.8 96.6 %all-gather.20.cloned.1.call-start = ((), (), s32[]{:S(2)}) async-start(), calls=%async_computation.16 | async-start | bytes 1966080 | tf_op jit(solution)/shard_map/while/body/eval_jaxpr/all_gather | solution.py:264
  1190.0 80.4 %all-gather.24.cloned.1.call-start = ((), (), s32[]{:S(2)}) async-start(), calls=%async_computation.18 | async-start | bytes 1769472 | tf_op jit(solution)/shard_map/while/body/eval_jaxpr/all_gather | solution.py:393
  1190.6 119.7 %reduce-scatter.20.cloned.1.call-start = ((), (), s32[]{:S(2)}) async-start(), calls=%async_computation.19 | async-start | bytes 1966080 | tf_op jit(solution)/shard_map/while/body/eval_jaxpr/reduce_scatter | solution.py:268
  1274.9 76.2 %all-gather.26.cloned.1.call-start = ((), (), s32[]{:S(2)}) async-start(), calls=%async_computation.20 | async-start | bytes 1966080 | tf_op jit(solution)/shard_map/while/body/eval_jaxpr/all_gather | solution.py:288
  1314.8 80.8 %reduce-scatter.22.cloned.1.call-start = ((), (), s32[]{:S(2)}) async-start(), calls=%async_computation.21 | async-start | bytes 1966080 | tf_op jit(solution)/shard_map/while/body/eval_jaxpr/reduce_scatter | solution.py:301
  1361.4 75.7 %all-gather.28.cloned.1.call-start = ((), (), s32[]{:S(2)}) async-start(), calls=%async_computation.22 | async-start | bytes 1966080 | tf_op jit(solution)/shard_map/while/body/eval_jaxpr/all_gather | solution.py:314
  1400.8 215.8 %reduce-scatter.26.cloned.1.call-start = ((), (), s32[]{:S(2)}) async-start(), calls=%async_computation.24 | async-start | bytes 1966080 | tf_op jit(solution)/shard_map/while/body/eval_jaxpr/reduce_scatter | solution.py:325
  1589.4 57.9 %reduce-scatter.30.cloned.1.call-start = ((), (), s32[]{:S(2)}) async-start(), calls=%async_computation.26 | async-start | bytes 1966080 | tf_op jit(solution)/shard_map/while/body/eval_jaxpr/reduce_scatter | solution.py:328
  1590.9 102.7 %reduce-scatter.38.cloned.1.call-start = ((), (), s32[]{:S(2)}) async-start(), calls=%async_computation.30 | async-start | bytes 2654208 | tf_op jit(solution)/shard_map/while/body/eval_jaxpr/reduce_scatter | solution.py:208
  1595.8 143.6 %reduce-scatter.36.cloned.1.call-start = ((), (), s32[]{:S(2)}) async-start(), calls=%async_computation.29 | async-start | bytes 2654208 | tf_op jit(solution)/shard_map/while/body/eval_jaxpr/reduce_scatter | solution.py:207
  1598.8 178.6 %reduce-scatter.34.cloned.1.call-start = ((), (), s32[]{:S(2)}) async-start(), calls=%async_computation.28 | async-start | bytes 884736 | tf_op jit(solution)/shard_map/while
  1602.2 213.3 %reduce-scatter.24.cloned.1.call-start = ((), (), s32[]{:S(2)}) async-start(), calls=%async_computation.23 | async-start | bytes 884736 | tf_op jit(solution)/shard_map/while/body/eval_jaxpr/reduce_scatter | solution.py:203
  1604.3 249.6 %reduce-scatter.28.cloned.1.call-start = ((), (), s32[]{:S(2)}) async-start(), calls=%async_computation.25 | async-start | bytes 884736 | tf_op jit(solution)/shard_map/while/body/eval_jaxpr/reduce_scatter | solution.py:204
  1619.1 272.9 %reduce-scatter.32.cloned.1.call-start = ((), (), s32[]{:S(2)}) async-start(), calls=%async_computation.27 | async-start | bytes 884736 | tf_op jit(solution)/shard_map/while/body/eval_jaxpr/reduce_scatter | solution.py:205
  1649.9 279.7 %reduce-scatter.40.cloned.1.call-start = ((), (), s32[]{:S(2)}) async-start(), calls=%async_computation.31 | async-start | bytes 1966080 | tf_op jit(solution)/shard_map/while/body/eval_jaxpr/reduce_scatter | solution.py:350
  1758.0 146.1 %copy-start.30 = (f32[384,192]{1,0:T(8,128)S(1)}, f32[384,192]{1,0:T(8,128)}, u32[]{:S(2)}) copy-start(f32[384,192]{1,0:T(8,128)} %get-tuple-element.2370) | copy-start | bytes 884740 | tf_op jit(solution)/shard_map/while
  1760.5 143.7 %copy-start.28 = (f32[384,192]{1,0:T(8,128)S(1)}, f32[384,192]{1,0:T(8,128)}, u32[]{:S(2)}) copy-start(f32[384,192]{1,0:T(8,128)} %get-tuple-element.2371) | copy-start | bytes 884740 | tf_op jit(solution)/shard_map/while
  1760.5 169.2 %copy-start.16 = (f32[256,768]{1,0:T(8,128)S(1)}, f32[256,768]{1,0:T(8,128)}, u32[]{:S(2)}) copy-start(f32[256,768]{1,0:T(8,128)} %get-tuple-element.2017) | copy-start | bytes 2359300 | tf_op jit(solution)/shard_map/while
  1760.7 170.7 %copy-start.72 = (f32[192]{0:T(256)}, f32[192]{0:T(256)S(1)}, u32[]{:S(2)}) copy-start(f32[192]{0:T(256)S(1)} %select_add_fusion.47) | copy-start | bytes 2308 | tf_op jit(solution)/shard_map/while
  (189 other events, 4627.8 us)
Sparse Core Ops, SparseCore 0:
  9.8 39.7 all-gather.13
  52.8 18.4 all-gather.17
  72.9 19.6 all-gather.15
  190.1 35.2 reduce-scatter.17
  226.9 21.7 all-gather.21
  250.1 37.0 all-gather.19
  288.8 21.6 all-gather.23
  315.0 35.2 reduce-scatter.19
  354.9 36.0 all-gather.25
  401.4 34.1 reduce-scatter.21
  440.9 36.0 all-gather.27
  629.5 26.9 reduce-scatter.25
  659.2 28.1 reduce-scatter.29
  691.0 42.4 reduce-scatter.37
  736.7 42.4 reduce-scatter.35
  782.2 34.9 reduce-scatter.33
  820.2 34.9 reduce-scatter.23
  858.6 35.0 reduce-scatter.27
  896.8 34.9 reduce-scatter.31
  933.9 35.2 reduce-scatter.39
  973.5 36.0 all-gather.13
  1012.8 18.5 all-gather.17
  1032.9 19.6 all-gather.15
  1150.2 35.2 reduce-scatter.17
  1187.1 21.7 all-gather.21
  1210.3 37.0 all-gather.19
  1248.8 21.6 all-gather.23
  1275.0 35.2 reduce-scatter.19
  1315.0 36.0 all-gather.25
  1361.5 34.1 reduce-scatter.21
  1400.9 36.0 all-gather.27
  1589.5 27.0 reduce-scatter.25
  1619.1 28.1 reduce-scatter.29
  1651.0 42.4 reduce-scatter.37
  1696.9 42.4 reduce-scatter.35
  1742.4 35.0 reduce-scatter.33
  1780.5 34.9 reduce-scatter.23
  1819.0 34.9 reduce-scatter.27
  1856.9 34.9 reduce-scatter.31
  1894.3 35.2 reduce-scatter.39
where the time goes:
time: 2020 us; the launch traced here: 1990 us
  waiting for transfers between devices  1120 us (55%)
  matrix products  281 us (14%)
  other arithmetic  226 us (11%)
  local copies, waits for them, and re-layouts  171 us (8%)
  blocking collectives  166 us (8%)
    dynamic_slice x128, local copies, waits for them, and re-layouts, key_block(): lax.dynamic_slice_in_dim(matrix, number * key_size, key_size, 0)  125 us
    reduce_scatter x2, waiting for transfers between devices, reduce_grads(): lax.psum_scatter(matrices[4], ('shard', 'ctx'), scatter_dimension=0, tile...  89.6 us
    reduce_scatter x2, waiting for transfers between devices, reduce_grads(): lax.psum_scatter(matrices[5], ('shard', 'ctx'), scatter_dimension=1, tile...  78.5 us
    all_gather x2, waiting for transfers between devices, micro_batch(): lax.all_gather(hidden.astype(jnp.bfloat16), 'tp', axis=0, tiled=True)  77.1 us
    reduce_scatter x2, waiting for transfers between devices, reduce_grads(): lax.psum_scatter(matrices[2], ('shard', 'ctx'), scatter_dimension=0, tile...  74.4 us
    reduce_scatter x2, waiting for transfers between devices, reduce_grads(): lax.psum_scatter(matrices[0], ('shard', 'ctx'), scatter_dimension=0, tile...  73.8 us
    all_gather x2, waiting for transfers between devices, micro_batch(): ffn_grad_block = lax.all_gather(ffn_grad, 'tp', axis=0, tiled=True)  72.4 us
    all_gather x2, waiting for transfers between devices, micro_batch(): mixer_grad_block = lax.all_gather(mixer_grad, 'tp', axis=0, tiled=True)  70.8 us
  transfers between devices with their start and end apart: 40, of which 38 were waited for; matrix products, arithmetic and copies ran while one was open for 5% of the time, Pallas kernels for 0%

commit v1 on v0

v1 whole, which is shorter than its diff:
```python
import functools

import jax
import jax.numpy as jnp
from jax import lax
from jax.experimental import pallas as pl
from jax.experimental.pallas import tpu as pltpu
from jax.sharding import PartitionSpec as P

HD = 64
EXT = 128
VE = 80
epsilon = 1e-12
f32 = jnp.float32
bf16 = jnp.bfloat16


def extended(block, extra_rows):
    n = block.shape[1]
    row = lax.broadcasted_iota(jnp.int32, (EXT - HD, n), 0)
    extra = jnp.zeros((EXT - HD, n), f32)
    for place, values in enumerate(extra_rows):
        extra = jnp.where(row == place, values, extra)
    return jnp.concatenate([block, extra.astype(bf16)], axis=0)


def key_bias(meta, block, size, blocks):
    count = meta[1 + blocks + block]
    lane = lax.broadcasted_iota(jnp.int32, (1, size), 1)
    return jnp.where(lane < count, 0.0, -1e30).astype(f32)


def forward_kernel(meta, qt, *refs, size, pieces, inner, unroll):
    kv = refs[:pieces]
    ot, lse, key_rows, value_cols, acc, top = refs[pieces:]
    blocks = pieces * inner
    n = qt.shape[1]
    one = jnp.ones((1, size), f32)
    for e in range(pieces):
        for j in range(inner):
            b = e * inner + j
            here = slice(j * size, (j + 1) * size)
            there = slice(b * size, (b + 1) * size)
            bias = key_bias(meta, b, size, blocks)
            key_rows[there, :] = extended(kv[e][:HD, here], [bias]).T
            value_cols[:, there] = extended(kv[e][HD:, here], [one])[:VE]
    queries = extended(qt[...], [jnp.ones((1, n), f32)])
    acc[...] = jnp.zeros_like(acc)
    top[...] = jnp.full_like(top, -1e30)

    def step(i, carry):
        starts = [pl.multiple_of(meta[1 + i * unroll + u] * size, size) for u in range(unroll)]
        scores = [
            jnp.dot(key_rows[pl.ds(s, size), :], queries, preferred_element_type=f32)
            for s in starts
        ]
        old = top[...]
        new = old
        for s in scores:
            new = jnp.maximum(new, jnp.max(s, axis=0, keepdims=True))
        total = acc[...] * jnp.exp(old - new)
        for s, start in zip(scores, starts):
            probs = jnp.exp(s - new).astype(bf16)
            total = total + jnp.dot(
                value_cols[:, pl.ds(start, size)], probs, preferred_element_type=f32
            )
        acc[...] = total
        top[...] = new
        return carry

    lax.fori_loop(0, (meta[0] + unroll - 1) // unroll, step, 0)
    exp_total = acc[HD : HD + 1, :]
    out = (acc[:HD, :] / exp_total).astype(bf16)
    for j in range(ot.shape[0]):
        ot[j] = out[:, j * ot.shape[2] : (j + 1) * ot.shape[2]]
    lse[0] = top[...] + jnp.log(exp_total)


def backward_kernel(meta, qt, ot, dot_t, lse, *refs, size, pieces, inner):
    kv = refs[:pieces]
    dq, keep, send = refs[pieces : pieces + 3]
    key_cols, value_cols, key_rows, query_rows, grad_rows, grad_cols, dq_acc = refs[pieces + 3 :]
    blocks = pieces * inner
    half = keep.shape[0]
    n = qt.shape[1]
    one = jnp.ones((1, size), f32)
    for e in range(pieces):
        for j in range(inner):
            b = e * inner + j
            here = slice(j * size, (j + 1) * size)
            there = slice(b * size, (b + 1) * size)
            bias = key_bias(meta, b, size, blocks)
            keys = extended(kv[e][:HD, here], [bias, one, one, one])
            key_cols[:, there] = keys
            key_rows[there, :] = keys.T
            value_cols[:, there] = extended(kv[e][HD:, here], [one, one])
    minus = -lse[0]
    high = minus.astype(bf16).astype(f32)
    mid = (minus - high).astype(bf16).astype(f32)
    query_rows[...] = extended(qt[...], [jnp.ones((1, n), f32), high, mid, minus - high - mid]).T
    grads = jnp.concatenate([dot_t[j] for j in range(dot_t.shape[0])], 1)
    outs = jnp.concatenate([ot[j] for j in range(ot.shape[0])], 1)
    grad_cols[...] = grads
    row_dot = -jnp.sum(grads.astype(f32) * outs.astype(f32), axis=0, keepdims=True)
    high = row_dot.astype(bf16).astype(f32)
    grad_rows[...] = extended(grads, [high, row_dot - high]).T
    dq_acc[...] = jnp.zeros_like(dq_acc)
    keep[...] = jnp.zeros_like(keep)
    send[...] = jnp.zeros_like(send)

    def step(i, carry):
        b = meta[1 + i]
        start = pl.multiple_of(b * size, size)
        probs = jnp.exp(
            jnp.dot(query_rows[...], key_cols[:, pl.ds(start, size)], preferred_element_type=f32)
        )
        centred = jnp.dot(
            grad_rows[...], value_cols[:, pl.ds(start, size)], preferred_element_type=f32
        )
        score_grad = (probs * centred).astype(bf16)
        dq_acc[...] += jnp.dot(
            score_grad, key_rows[pl.ds(start, size), :], preferred_element_type=f32
        )
        dk = jnp.dot(qt[...], score_grad, preferred_element_type=f32).astype(bf16)
        dv = jnp.dot(grad_cols[...], probs.astype(bf16), preferred_element_type=f32).astype(bf16)
        lane = pl.multiple_of((b % inner) * size, size)
        piece = b // inner

        @pl.when(piece < half)
        def _():
            keep[piece, :HD, pl.ds(lane, size)] = dk
            keep[piece, HD:, pl.ds(lane, size)] = dv

        @pl.when(piece >= half)
        def _():
            send[piece - half, :HD, pl.ds(lane, size)] = dk
            send[piece - half, HD:, pl.ds(lane, size)] = dv

        return carry

    lax.fori_loop(0, meta[0], step, 0)
    dq[...] = (dq_acc[...].T[:HD] * HD ** (-0.5)).astype(bf16)


def attend_forward(meta, qt, kvs, size, first, count):
    n, pieces = qt.shape[1], len(kvs)
    columns = kvs[0].shape[1]
    inner = columns // size
    keys = pieces * columns
    unroll = 2 if (pieces * inner) % 2 == 0 else 1
    return pl.pallas_call(
        functools.partial(
            forward_kernel, size=size, pieces=pieces, inner=inner, unroll=unroll
        ),
        grid_spec=pltpu.PrefetchScalarGridSpec(
            num_scalar_prefetch=1,
            grid=(count,),
            in_specs=[pl.BlockSpec((HD, n), lambda h, m: (first + h, 0))]
            + [pl.BlockSpec((2 * HD, columns), lambda h, m: (first + h, 0))] * pieces,
            out_specs=[
                pl.BlockSpec((n // size, HD, size), lambda h, m: (0, h, 0)),
                pl.BlockSpec((1, 1, n), lambda h, m: (h, 0, 0)),
            ],
            scratch_shapes=[
                pltpu.VMEM((keys, EXT), bf16),
                pltpu.VMEM((VE, keys), bf16),
                pltpu.VMEM((VE, n), f32),
                pltpu.VMEM((1, n), f32),
            ],
        ),
        out_shape=[
            jax.ShapeDtypeStruct((n // size, count * HD, size), bf16),
            jax.ShapeDtypeStruct((count, 1, n), f32),
        ],
        cost_estimate=pl.CostEstimate(
            flops=20 * count * HD * n * keys,
            bytes_accessed=8 * count * HD * n,
            transcendentals=0,
        ),
        name="attend_forward",
    )(meta, qt, *kvs)


def attend_backward(meta, qt, ot, dot_t, lse, kvs, size, first, count, seq):
    n, pieces = qt.shape[1], len(kvs)
    columns = kvs[0].shape[1]
    inner = columns // size
    keys = pieces * columns
    half = (pieces + 1) // 2
    row_spec = pl.BlockSpec((HD, n), lambda h, m: (first + h, 0))
    split_spec = pl.BlockSpec((n // size, HD, size), lambda h, m: (0, first + h, 0))
    grad_spec = pl.BlockSpec((n // size, HD, size), lambda h, m: (0, first + h, seq))
    part_spec = pl.BlockSpec((half, 2 * HD, columns), lambda h, m: (0, h, 0))
    part_shape = jax.ShapeDtypeStruct((half, 2 * HD * count, columns), bf16)
    return pl.pallas_call(
        functools.partial(backward_kernel, size=size, pieces=pieces, inner=inner),
        grid_spec=pltpu.PrefetchScalarGridSpec(
            num_scalar_prefetch=1,
            grid=(count,),
            in_specs=[row_spec, split_spec, grad_spec]
            + [pl.BlockSpec((1, 1, n), lambda h, m: (first + h, 0, 0))]
            + [pl.BlockSpec((2 * HD, columns), lambda h, m: (first + h, 0))] * pieces,
            out_specs=[pl.BlockSpec((HD, n), lambda h, m: (h, 0)), part_spec, part_spec],
            scratch_shapes=[
                pltpu.VMEM((EXT, keys), bf16),
                pltpu.VMEM((EXT, keys), bf16),
                pltpu.VMEM((keys, EXT), bf16),
                pltpu.VMEM((n, EXT), bf16),
                pltpu.VMEM((n, EXT), bf16),
                pltpu.VMEM((HD, n), bf16),
                pltpu.VMEM((n, EXT), f32),
            ],
        ),
        out_shape=[jax.ShapeDtypeStruct((count * HD, n), bf16), part_shape, part_shape],
        cost_estimate=pl.CostEstimate(
            flops=count * HD * n,
            bytes_accessed=count * HD * n,
            transcendentals=0,
        ),
        name="attend_backward",
    )(meta, qt, ot, dot_t, lse, *kvs)


def pair_kernel(left_a, right_a, left_b, right_b, out):
    for place, left, right in ((0, left_a, right_a), (1, left_b, right_b)):

        @pl.when(pl.program_id(0) == place)
        def _():
            out[0] = lax.dot_general(
                left[...], right[...], (((0,), (0,)), ((), ())), preferred_element_type=f32
            ).astype(bf16)


def weight_grad_pair(left_a, right_a, left_b, right_b, tile):
    n, columns = left_a.shape
    tiles = columns // tile
    width = right_a.shape[1]
    whole = pl.BlockSpec((n, width), lambda g, i: (0, 0))
    return pl.pallas_call(
        pair_kernel,
        grid=(2, tiles),
        in_specs=[
            pl.BlockSpec((n, tile), lambda g, i: (0, i * (1 - g) + (tiles - 1) * g)),
            whole,
            pl.BlockSpec((n, tile), lambda g, i: (0, i * g)),
            whole,
        ],
        out_specs=pl.BlockSpec((1, tile, width), lambda g, i: (g, i, 0)),
        out_shape=jax.ShapeDtypeStruct((2, columns, width), bf16),
        cost_estimate=pl.CostEstimate(
            flops=4 * n * columns * width, bytes_accessed=8 * n * columns, transcendentals=0
        ),
        name="weight_grad_pair",
    )(left_a, right_a, left_b, right_b)


def swap(x, axis, bits):
    return lax.ppermute(x, axis, [(i, i ^ bits) for i in range(lax.axis_size(axis))])


def wide(x):
    return x.astype(f32)


def low(x):
    return x.astype(bf16)


def dot(a, b, contract):
    return lax.dot_general(a, b, (contract, ((), ())), preferred_element_type=f32)


NN = ((1,), (0,))
NT = ((1,), (1,))
TN = ((0,), (0,))


def xor_order(x, axis, index):
    n = x.shape[axis]
    bit = 1
    while bit < n:
        moved = jnp.stack([lax.index_in_dim(x, i ^ bit, axis, False) for i in range(n)], axis)
        x = jnp.where((index & bit) != 0, moved, x)
        bit *= 2
    return x


def norm_forward(resid, gain, shift):
    centre = resid - jnp.mean(resid, axis=-1, keepdims=True)
    factor = lax.rsqrt(jnp.mean(centre * centre, axis=-1, keepdims=True) + epsilon)
    normed = centre * factor
    return (normed * gain + shift, normed, factor)


def norm_backward(grad_out, normed, factor, gain):
    scaled = grad_out * gain
    centred = scaled - jnp.mean(scaled, axis=-1, keepdims=True)
    return factor * (centred - normed * jnp.mean(scaled * normed, axis=-1, keepdims=True))


def on_device(
    tokens,
    cotangent,
    lengths,
    query_weight,
    query_bias,
    key_weight,
    value_weight,
    value_bias,
    out_weight,
    out_bias,
    first_gain,
    first_shift,
    up_weight,
    up_bias,
    down_weight,
    down_bias,
    second_gain,
    second_shift,
):
    shard_n, ctx_n, tp_n = (lax.axis_size(a) for a in ("shard", "ctx", "tp"))
    shard_i, ctx_i, tp_i = (lax.axis_index(a) for a in ("shard", "ctx", "tp"))
    seqs, rows, model = tokens.shape
    part = model // shard_n
    width = query_weight.shape[1]
    heads = width // HD
    units = up_weight.shape[1]
    quarter = units // ctx_n
    two = shard_n == 2
    first = shard_i == 0

    def flip(x):
        if not two:
            return x
        return jnp.where(first, x, jnp.concatenate([x[..., part:], x[..., :part]], -1))

    def gather_local(x):
        if two:
            return jnp.concatenate([x, swap(x, "shard", 1)], -1)
        return lax.all_gather(x, "shard", axis=x.ndim - 1, tiled=True)

    def scatter_local(x):
        if two:
            return wide(x[:, :part]) + wide(swap(x[:, part:], "shard", 1))
        return wide(lax.psum_scatter(x, "shard", scatter_dimension=1, tiled=True))

    def after(x, *gates):
        return lax.optimization_barrier((x, *gates))[0]

    bits = ctx_n.bit_length() - 1
    ctx_bits = [1 << i for i in reversed(range(bits))]

    def bit_reverse(e):
        return sum(((e >> i) & 1) << (bits - 1 - i) for i in range(bits))

    ctx_order = [bit_reverse(e) for e in range(ctx_n)]
    half = (ctx_n + 1) // 2

    def exchange(x):
        return lax.all_to_all(x, "tp", 0, 0, tiled=True)

    def tp_gather(x):
        return exchange(jnp.broadcast_to(x[None], (tp_n, *x.shape)))

    def ctx_gather(chunks):
        for bit in ctx_bits:
            chunks = chunks + [swap(c, "ctx", bit) for c in chunks]
        return chunks

    kv_t = jnp.stack(
        [key_weight.T.reshape(heads, HD, part), value_weight.T.reshape(heads, HD, part)], 1
    ).reshape(2 * width, part)
    mine = lambda w: lax.dynamic_slice_in_dim(w, ctx_i * quarter, quarter, 0)
    weights = jnp.concatenate(
        [query_weight.T, kv_t, mine(up_weight.T), mine(down_weight), out_weight], 0
    )
    weights = flip(gather_local(weights))
    qkv_t = weights[: 3 * width]
    up_down = weights[3 * width : 3 * width + 2 * quarter].reshape(2, quarter, model)
    out_own = weights[3 * width + 2 * quarter :]

    first_in = tp_gather(tokens[0])
    bias_rows = []
    rest = up_bias
    for _ in range(3):
        bias_rows.append(low(rest))
        rest = rest - wide(bias_rows[-1])
    bias_rows = jnp.stack(bias_rows, 0)
    extra = units * 3 // model
    fill = -(width + extra) % 16
    out_own = jnp.concatenate(
        [out_own, bias_rows.reshape(extra, model), jnp.zeros((fill, model), bf16)], 0
    )
    blocks = [first_in.reshape(tp_n * rows, model)]
    for s in range(1, seqs):
        blocks.append(tp_gather(after(tokens[s], blocks[-1])).reshape(tp_n * rows, model))
    out_all = tp_gather(after(out_own, blocks[-1]))
    kv_bias = jnp.stack(
        [jnp.zeros((heads, HD), f32), value_bias.reshape(heads, HD)], 1
    ).reshape(2 * width, 1)
    up_down = lax.all_gather(after(up_down, first_in), ("ctx", "tp"), axis=1, tiled=True)
    up_full, down_full = up_down[0], up_down[1]
    out_full = out_all[:, :width].reshape(tp_n * width, model)
    unit_bias = wide(out_all[:, width : width + extra]).reshape(tp_n, 3, ctx_n, quarter)
    unit_bias = (unit_bias[:, 0] + unit_bias[:, 1]) + unit_bias[:, 2]
    unit_bias = unit_bias.transpose(1, 0, 2).reshape(1, ctx_n * tp_n * quarter)

    place = jnp.arange(ctx_n * tp_n)
    order = bit_reverse((place // tp_n) ^ ctx_i) * tp_n + place % tp_n
    block_at = (bit_reverse(place // tp_n) ^ ctx_i) * tp_n + place % tp_n

    def project(s, block):
        kv = low(dot(qkv_t[width:], block, NT) + kv_bias)
        q = low(dot(qkv_t[:width], block, NT) + query_bias[:, None])
        return kv, q * bf16(HD ** (-0.5))

    def ctx_pieces(kv, gate):
        chunks = [kv]
        for bit in ctx_bits:
            chunks = chunks + [swap(c, "ctx", bit) for c in chunks]
            if gate is not None and bit == ctx_bits[0]:
                chunks = [after(c, gate) for c in chunks]
        return chunks

    metas = []
    for s in range(seqs):
        count = jnp.clip(lengths[s] - block_at * rows, 0, rows)
        metas.append(
            jnp.concatenate([((lengths[s] + rows - 1) // rows)[None], order, count]).astype(
                jnp.int32
            )
        )

    outs, totals, attended, queries, keys_values = [], [], [], [], []
    kv, q = project(0, blocks[0])
    kvs = ctx_pieces(kv, None)
    for s in range(seqs):
        keys_values.append(kvs)
        queries.append(q)
        if s + 1 < seqs and heads > 1:
            ot_a, lse_a = attend_forward(metas[s], q, kvs, rows, 0, heads - 1)
            kv_next, q_next = project(s + 1, after(blocks[s + 1], lse_a))
            meta = after(metas[s], kv_next, q_next)
            ot_b, lse_b = attend_forward(meta, q, kvs, rows, heads - 1, 1)
            ot = jnp.concatenate([ot_a, ot_b], 1)
            lse = jnp.concatenate([lse_a, lse_b], 0)
            q, kvs = q_next, ctx_pieces(kv_next, lse_b)
            ot = after(ot, out_all)
        else:
            ot, lse = attend_forward(metas[s], q, kvs, rows, 0, heads)
        outs.append(ot)
        totals.append(lse)
        attended.append(exchange(ot).reshape(tp_n * width, rows))
    attended_t = jnp.concatenate(attended, 1)

    flat = wide(tokens.reshape(seqs * rows, model))
    cot = wide(cotangent.reshape(seqs * rows, model))
    mixed = dot(attended_t, out_full, TN) + out_bias
    hidden, normed_1, factor_1 = norm_forward(flat + mixed, first_gain, first_shift)
    hidden_low = low(hidden)
    pre = dot(hidden_low, up_full, NT) + unit_bias
    share = 0.5 * (1.0 + lax.erf(pre * 0.5**0.5))
    activated = low(pre * share)
    slope = low(share + pre * jnp.exp(-0.5 * pre * pre) * 0.3989422804014327)
    ffn_out = dot(activated, down_full, NN) + down_bias
    result, normed_2, factor_2 = norm_forward(hidden + ffn_out, second_gain, second_shift)
    here = (ctx_i * tp_n + tp_i) * rows + jnp.arange(rows)
    valid = (here[None, :] < lengths[:, None]).reshape(seqs * rows, 1)
    grad_result = jnp.where(valid, cot, 0.0)
    gain_2_grad = jnp.sum(grad_result * normed_2, axis=0)
    shift_2_grad = jnp.sum(grad_result, axis=0)
    grad_second = norm_backward(grad_result, normed_2, factor_2, second_gain)
    ffn_grad = low(grad_second)
    bias_d_grad = jnp.sum(wide(ffn_grad), axis=0)
    pre_grad = low(dot(ffn_grad, down_full, NT) * wide(slope))
    grad_hidden = grad_second + dot(pre_grad, up_full, NN)
    up_bias_grad = jnp.sum(wide(pre_grad), axis=0)
    gain_1_grad = jnp.sum(grad_hidden * normed_1, axis=0)
    shift_1_grad = jnp.sum(grad_hidden, axis=0)
    grad_first = norm_backward(grad_hidden, normed_1, factor_1, first_gain)
    mixer_grad = low(grad_first)
    bias_o_grad = jnp.sum(wide(mixer_grad), axis=0)
    attended_grad_t = low(dot(out_full, mixer_grad, NT))
    value_bias_parts = jnp.sum(
        wide(attended_grad_t).reshape(tp_n, width, seqs * rows), axis=2
    )
    value_bias_grad = value_bias_parts.reshape(-1)
    up_bias_full = up_bias_grad.reshape(ctx_n, tp_n, quarter).transpose(1, 0, 2).reshape(-1)
    vectors = [
        value_bias_grad,
        bias_o_grad,
        gain_1_grad,
        shift_1_grad,
        up_bias_full,
        bias_d_grad,
        gain_2_grad,
        shift_2_grad,
    ]
    sizes = [v.shape[0] for v in vectors]
    summed = 0.0
    for i, v in enumerate(vectors):
        summed = summed + jnp.pad(v, (sum(sizes[:i]), sum(sizes[i + 1 :])))

    def all_sum(x, axis):
        n = lax.axis_size(axis)
        if n & (n - 1):
            return lax.psum(x, axis)
        for i in range(n.bit_length() - 1):
            x = x + swap(x, axis, 1 << i)
        return x


    grad_cols = exchange(attended_grad_t.reshape(tp_n, width, seqs * rows))

    def sum_ctx(x):
        for bit in reversed(ctx_bits):
            x = low(x)
            x = wide(x) + wide(swap(x, "ctx", bit))
        return x

    late_pre = after(pre_grad, attended_grad_t)
    ffn_grads = weight_grad_pair(late_pre, hidden_low, activated, ffn_grad, quarter * ctx_n)
    ffn_sum = lax.psum_scatter(ffn_grads, ("ctx", "tp"), scatter_dimension=1, tiled=True)
    out_grad = low(dot(attended_t, mixer_grad, NN))

    grad_rows = grad_first.reshape(seqs, rows, model)
    spans = []
    for s in range(seqs):
        if s + 1 < seqs or heads == 1:
            spans.append((s, 0, heads))
        else:
            spans += [(s, 0, heads - 1), (s, heads - 1, 1)]
    near = ctx_bits[-1:]
    far = list(reversed(ctx_bits[:-1]))

    def near_sum(keep, send):
        total = wide(keep)
        for bit in near:
            total = total + wide(swap(send, "ctx", bit))
        return [low(total[p]) for p in range(half)]

    def far_sum(chunks):
        for bit in far:
            n = len(chunks) // 2
            chunks = [
                low(wide(a) + wide(swap(b, "ctx", bit))) for a, b in zip(chunks[:n], chunks[n:])
            ]
        return chunks[0]

    def tp_sum(x):
        x = exchange(x.reshape(tp_n, x.shape[0] // tp_n, x.shape[1]))
        return jnp.sum(wide(x), axis=0)

    qkv_grad = 0.0
    sums = 0.0
    input_parts = []
    dq_parts = [[] for _ in range(seqs)]
    dkv_parts = [[] for _ in range(seqs)]
    last = ()
    near_chunks = None
    number = 0

    def finish(s):
        grads_t = jnp.concatenate(dq_parts[s] + dkv_parts[s], 0)
        back = low(dot(grads_t, qkv_t, TN))
        return (
            back,
            low(
                grad_rows[s]
                + wide(lax.psum_scatter(back, "tp", scatter_dimension=0, tiled=True))
            ),
            dot(grads_t, blocks[s], NN),
            jnp.sum(wide(jnp.concatenate(dq_parts[s], 0)), axis=1),
        )

    def take(done):
        return (input_parts + [done[1]], qkv_grad + done[2], sums + done[3])

    for s, start, count in spans:
        meta = metas[s]
        wait = list(last) if last else [grad_cols]
        if number >= 1:
            wait += near_chunks
        if number == 1:
            out_grad = low(scatter_local(flip(out_grad)))
            wait += [out_grad]
        if number >= 2:
            done_s = spans[number - 2][0]
            wait.append(dkv_parts[done_s][-1])
            if spans[number - 1][0] != done_s:
                done = finish(done_s)
                wait.append(done[0])
                input_parts, qkv_grad, sums = take(done)
            if number == 2:
                out_grad = tp_sum(out_grad)
                summed = all_sum(summed, "tp")
                wait += [out_grad, summed]
        if wait:
            meta = after(meta, *wait)
        dq, keep, send = attend_backward(
            meta, queries[s], outs[s], grad_cols, totals[s], keys_values[s], rows, start, count, s
        )
        last = (dq,)
        number += 1
        near_chunks = near_sum(keep, send)
        dq_parts[s].append(dq)
        dkv_parts[s].append(far_sum(near_chunks))
    if number == 1:
        out_grad = low(scatter_local(flip(out_grad)))
    if number <= 2:
        out_grad = tp_sum(out_grad)
        summed = all_sum(summed, "tp")
    summed = all_sum(all_sum(summed, "ctx"), "shard")
    input_parts, qkv_grad, sums = take(finish(seqs - 1))
    input_grads = jnp.stack(input_parts, 0)
    out_sum = sum_ctx(out_grad)

    ffn_sum = scatter_local(flip(ffn_sum.reshape(2 * quarter, model)))
    chunks = ctx_gather([low(ffn_sum)])
    stacked = jnp.stack([chunks[ctx_order.index(e)] for e in range(ctx_n)], 0)
    stacked = wide(xor_order(stacked, 0, ctx_i))
    up_sum = stacked[:, :quarter].reshape(units, part)
    down_sum = stacked[:, quarter:].reshape(units, part)

    qkv_sum = sum_ctx(scatter_local(flip(low(qkv_grad))))
    query_sum = qkv_sum[:width]
    kv_sum = qkv_sum[width:].reshape(heads, 2, HD, part)
    key_sum = kv_sum[:, 0].reshape(width, part)
    value_sum = kv_sum[:, 1].reshape(width, part)

    query_bias_sum = all_sum(all_sum(sums, "ctx"), "shard")
    query_bias_full = tp_gather(query_bias_sum).reshape(-1)
    ends = []
    at = 0
    for n in sizes:
        ends.append(summed[at : at + n])
        at += n
    return (
        low(result).reshape(seqs, rows, model),
        input_grads,
        query_sum.T,
        query_bias_full,
        key_sum.T,
        value_sum.T,
        ends[0],
        out_sum,
        ends[1],
        ends[2],
        ends[3],
        up_sum.T,
        ends[4],
        down_sum,
        ends[5],
        ends[6],
        ends[7],
    )


def solution(mesh):
    placed = (
        P("shard", ("ctx", "tp"), None),
        P("shard", ("ctx", "tp"), None),
        P("shard"),
        P("shard", "tp"),
        P("tp"),
        P("shard", "tp"),
        P("shard", "tp"),
        P("tp"),
        P("tp", "shard"),
        P(),
        P(),
        P(),
        P("shard", "tp"),
        P("tp"),
        P("tp", "shard"),
        P(),
        P(),
        P(),
    )
    return jax.shard_map(
        on_device,
        mesh=mesh,
        in_specs=placed,
        out_specs=(
            P("shard", ("ctx", "tp"), None),
            P("shard", ("ctx", "tp"), None),
            P("shard", "tp"),
            P(),
            P("shard", "tp"),
            P("shard", "tp"),
            P(),
            P("tp", "shard"),
            P(),
            P(),
            P(),
            P("shard", "tp"),
            P(),
            P("tp", "shard"),
            P(),
            P(),
            P(),
        ),
        check_vma=False,
    )
```

time: 2020 us -> 506 us (0.25); the launches traced: 1990 us -> 503 us
  waiting for transfers between devices: 1120 us -> 186 us
  matrix products: 281 us -> 42.6 us
  other arithmetic: 226 us -> 29.7 us
  blocking collectives: 166 us -> 0 us
  local copies, waits for them, and re-layouts: 171 us -> 31.3 us
  Pallas kernels: 0 us -> 139 us
  starting transfers between devices: 1.66 us -> 57.2 us
    reduce_scatter x22 -> x3, waiting for transfers between devices: 704 us -> 0.01 us  [the longest x2 0.01 us: finish(): lax.psum_scatter(back, 'tp', scatter_dimension=0, tiled=True)]
    all_gather x16 -> x1, waiting for transfers between devices: 379 us -> 0.02 us  [on_device(): lax.all_gather(after(up_down, first_in), ('ctx', 'tp'), axis=1, tiled=True)]
    dot_general x258 -> x15, matrix products: 275 us -> 42.6 us  [dot(): lax.dot_general(a, b, (contract, ((), ())), preferred_element_type=f32)]
    pallas_call x0 -> x7, Pallas kernels: none -> 139 us  [the longest x3 75 us: attend_backward(): pl.pallas_call(functools.partial(backward_kernel, size=size, pieces=piece...]
    dynamic_slice x140 -> x0, local copies, waits for them, and re-layouts: 131 us -> none  [the longest x128 125 us: key_block(): lax.dynamic_slice_in_dim(matrix, number * key_size, key_size, 0)]
    all_gather x20 -> x0, blocking collectives: 125 us -> none  [the longest x2 15.3 us: reduce_grads(): lax.all_gather(pieces[5].astype(jnp.bfloat16), 'ctx', axis=1, tiled=True)]
    ppermute x0 -> x31, waiting for transfers between devices: none -> 111 us  [swap(): lax.ppermute(x, axis, [(i, i ^ bits) for i in range(lax.axis_size(axis))])]
    all_to_all x0 -> x8, waiting for transfers between devices: none -> 75 us  [exchange(): return lax.all_to_all(x, 'tp', 0, 0, tiled=True)]
  transfers between devices with their start and end apart: 40 -> 43, of which waited for: 38 -> 20; matrix products, arithmetic and copies ran while one was open for 5% -> 14% of each run, Pallas kernels for 0% -> 25%
where the time goes in v1:
time: 506 us; the launch traced here: 503 us
  waiting for transfers between devices  186 us (37%)
  Pallas kernels  139 us (27%)
  starting transfers between devices  57.2 us (11%)
  matrix products  42.6 us (8%)
  local copies, waits for them, and re-layouts  31.3 us (6%)
  other arithmetic  29.7 us (6%)
  between operations  16.7 us (3%)
    ppermute x31, waiting for transfers between devices, swap(): lax.ppermute(x, axis, [(i, i ^ bits) for i in range(lax.axis_size(axis))])  111 us
    all_to_all x8, waiting for transfers between devices, exchange(): return lax.all_to_all(x, 'tp', 0, 0, tiled=True)  75 us
    pallas_call x3, Pallas kernels, attend_backward(): pl.pallas_call(functools.partial(backward_kernel, size=size, pieces=piece...  75 us
    pallas_call x3, Pallas kernels, attend_forward(): pl.pallas_call(functools.partial(forward_kernel, size=size, pieces=pieces...  52.3 us
    dot_general x15, matrix products, dot(): lax.dot_general(a, b, (contract, ((), ())), preferred_element_type=f32)  42.6 us
    all_to_all x8, starting transfers between devices, exchange(): return lax.all_to_all(x, 'tp', 0, 0, tiled=True)  33.2 us
    ppermute x31, starting transfers between devices, swap(): lax.ppermute(x, axis, [(i, i ^ bits) for i in range(lax.axis_size(axis))])  23.7 us
    pallas_call x1, Pallas kernels, weight_grad_pair(): pl.pallas_call(pair_kernel, grid=(2, tiles), in_specs=[pl.BlockSpec((n, t...  11.9 us
  transfers between devices with their start and end apart: 43, of which 20 were waited for; matrix products, arithmetic and copies ran while one was open for 14% of the time, Pallas kernels for 25%

profile of v1, /device:TPU:0, one launch (start us, length us, event | category | flops | bytes accessed | tf_op | source)
XLA Modules:
  0.0 502.6 jit_solution(14112099088103336701)
XLA Ops:
  7.2 2.0 slice_bitcast_fusion.15
  10.5 6.4 %all-to-all-start = ((bf16[4,256,768]{2,1,0:T(8,128)(2,1)}), bf16[4,256,768]{2,1,0:T(8,128)(2,1)S(1)}, u32[]{:S(2)}, u32[]{:S(2)}) async-start(bf16[4,256,768]{2,1,0:T(8,128)(2,1)} %broadcast_in_dim.30), calls=%async_computation | async-start | bytes 3145728 | tf_op jit(solution)/shard_map/all_to_all | solution.py:360
  23.2 19.9 %collective-permute-done = bf16[1152,384]{1,0:T(8,128)(2,1)} collective-permute-done((bf16[1152,384]{1,0:T(8,128)(2,1)}, bf16[1152,384]{1,0:T(8,128)(2,1)}, u32[]{:S(2)}, u32[]{:S(2)}) %collective-permute-start) | collective-permute-done | bytes 884768 | tf_op jit(solution)/shard_map/ppermute | solution.py:258
  43.1 2.5 maximum_select_fusion
  46.5 7.4 %all-to-all-done = bf16[4,256,768]{2,1,0:T(8,128)(2,1)S(1)} async-done(((bf16[4,256,768]{2,1,0:T(8,128)(2,1)}), bf16[4,256,768]{2,1,0:T(8,128)(2,1)S(1)}, u32[]{:S(2)}, u32[]{:S(2)}) %all-to-all-start) | async-done | bytes 1572896 | tf_op jit(solution)/shard_map/all_to_all | solution.py:360
  58.6 4.5 all-to-all-start.1
  63.1 17.8 %collective-permute-done.1.refs_1_ = bf16[384,1024]{1,0:T(8,128)(2,1)} collective-permute-done((bf16[384,1024]{1,0:T(8,128)(2,1)}, bf16[384,1024]{1,0:T(8,128)(2,1)}, u32[]{:S(2)}, u32[]{:S(2)}) %collective-permute-start.1) | collective-permute-done | bytes 786464 | tf_op jit(solution)/shard_map/ppermute | solution.py:258
  86.2 19.3 %attend_forward.3 = (bf16[4,128,256]{2,1,0:T(8,128)(2,1)}, f32[2,1,1024]{2,1,0:T(1,128)}) custom-call(s32[33]{0:T(128)} %get-tuple-element.57.meta, bf16[192,1024]{1,0:T(8,128)(2,1)} %fusion.15.qt, bf16[384,1024]{1,0:T(8,128)(2,1)} %add_convert_fusion.6.refs_0_, bf16[384,1024]{1,0:T(8,128)(2,1)} %collective-permute-done.1.refs_1_, ...), custom_call_target="tpu_custom_call" | custom-call | flops 10737418240 | bytes 1048576 | tf_op jit(solution)/shard_map/attend_forward/pallas_call | solution.py:151
  105.6 12.7 %all-to-all-done.1 = bf16[4,256,768]{2,1,0:T(8,128)(2,1)} async-done(((bf16[4,256,768]{2,1,0:T(8,128)(2,1)}), bf16[4,256,768]{2,1,0:T(8,128)(2,1)}, u32[]{:S(2)}, u32[]{:S(2)}) %all-to-all-start.1) | async-done | bytes 1572896 | tf_op jit(solution)/shard_map/all_to_all | solution.py:360
  118.2 2.2 add_convert_fusion.5.refs_0_
  121.1 2.9 fusion.14.qt
  123.9 11.1 %attend_forward.4 = (bf16[4,64,256]{2,1,0:T(8,128)(2,1)}, f32[1,1,1024]{2,1,0:T(1,128)}) custom-call(s32[33]{0:T(128)} %get-tuple-element.57.meta, bf16[192,1024]{1,0:T(8,128)(2,1)} %fusion.15.qt, bf16[384,1024]{1,0:T(8,128)(2,1)} %add_convert_fusion.6.refs_0_, bf16[384,1024]{1,0:T(8,128)(2,1)} %collective-permute-done.1.refs_1_, ...), custom_call_target="tpu_custom_call" | custom-call | flops 5368709120 | bytes 524288 | tf_op jit(solution)/shard_map/attend_forward/pallas_call | solution.py:151
  135.0 22.4 %collective-permute-done.4.refs_1_ = bf16[384,1024]{1,0:T(8,128)(2,1)} collective-permute-done((bf16[384,1024]{1,0:T(8,128)(2,1)S(1)}, bf16[384,1024]{1,0:T(8,128)(2,1)}, u32[]{:S(2)}, u32[]{:S(2)}) %collective-permute-start.4) | collective-permute-done | bytes 786464 | tf_op jit(solution)/shard_map/ppermute | solution.py:258
  159.0 3.5 all-to-all-start.2
  162.6 21.9 %attend_forward.5 = (bf16[4,192,256]{2,1,0:T(8,128)(2,1)}, f32[3,1,1024]{2,1,0:T(1,128)}) custom-call(s32[33]{0:T(128)} %get-tuple-element.66.meta, bf16[192,1024]{1,0:T(8,128)(2,1)} %fusion.14.qt, bf16[384,1024]{1,0:T(8,128)(2,1)} %copy-done.7, bf16[384,1024]{1,0:T(8,128)(2,1)} %collective-permute-done.4.refs_1_, ...), custom_call_target="tpu_custom_call" | custom-call | flops 16106127360 | bytes 1572864 | tf_op jit(solution)/shard_map/attend_forward/pallas_call | solution.py:151
  184.5 18.5 %all-to-all-done.2 = bf16[4,208,768]{2,1,0:T(8,128)(2,1)S(1)} async-done(((bf16[4,208,768]{2,1,0:T(8,128)(2,1)}), bf16[4,208,768]{2,1,0:T(8,128)(2,1)S(1)}, u32[]{:S(2)}, u32[]{:S(2)}) %all-to-all-start.2) | async-done | bytes 1277984 | tf_op jit(solution)/shard_map/all_to_all | solution.py:360
  203.0 3.5 all-to-all-start.4
  208.4 10.2 %all-to-all-done.4 = bf16[4,192,256]{2,1,0:T(8,128)(2,1)S(1)} async-done(((bf16[4,192,256]{2,1,0:T(8,128)(2,1)}), bf16[4,192,256]{2,1,0:T(8,128)(2,1)S(1)}, u32[]{:S(2)}, u32[]{:S(2)}) %all-to-all-start.4) | async-done | bytes 393248 | tf_op jit(solution)/shard_map/all_to_all | solution.py:360
  218.6 4.1 all-to-all-start.3
  225.5 8.6 %all-to-all-done.3 = bf16[4,192,256]{2,1,0:T(8,128)(2,1)} async-done(((bf16[4,192,256]{2,1,0:T(8,128)(2,1)}), bf16[4,192,256]{2,1,0:T(8,128)(2,1)}, u32[]{:S(2)}, u32[]{:S(2)}) %all-to-all-start.3) | async-done | bytes 393248 | tf_op jit(solution)/shard_map/all_to_all | solution.py:360
  234.1 2.5 fusion.47
  237.8 6.4 %multiply_convert_fusion.1 = (bf16[512,3072]{1,0:T(8,128)(2,1)S(1)}, f32[512,3072]{1,0:T(8,128)S(1)}) fusion(f32[3072]{0:T(1024)} %add.308, bf16[512,768]{1,0:T(8,128)(2,1)S(1)} %fusion.11.right_a, bf16[2,3072,768]{2,1,0:T(8,128)(2,1)} %all-gather.2.cloned.1.call-done), kind=kOutput, calls=%fused_computation.8 | convolution fusion | flops 2425356288 | bytes 14954496 | tf_op jit(solution)/shard_map/dot_general | solution.py:270
  244.3 2.7 fusion.48
  250.1 6.1 %convert_reduce_fusion = (f32[3072]{0:T(1024)}, bf16[512,3072]{1,0:T(8,128)(2,1)S(1)}) fusion(f32[512,3072]{1,0:T(8,128)S(1)} %get-tuple-element.186, f32[3072]{0:T(1024)S(1)} %copy-done.40, bf16[512,768]{1,0:T(8,128)(2,1)S(1)} %get-tuple-element.150.right_b, bf16[2,3072,768]{2,1,0:T(8,128)(2,1)S(1)} %copy-done.51), kind=kOutput, calls=%fused_computation.6 | convolution fusion | flops 2439508992 | bytes 14966784 | tf_op jit(solution)/shard_map/dot_general | solution.py:270
  256.1 3.5 multiply_reduce_fusion.1
  261.0 2.3 convert_reduce_fusion.3
  263.3 11.9 %weight_grad_pair.1 = bf16[2,3072,768]{2,1,0:T(8,128)(2,1)} custom-call(bf16[512,3072]{1,0:T(8,128)(2,1)} %copy-done.56, bf16[512,768]{1,0:T(8,128)(2,1)} %copy-done.16, bf16[512,3072]{1,0:T(8,128)(2,1)} %copy-done.55, bf16[512,768]{1,0:T(8,128)(2,1)} %copy-done.13), custom_call_target="tpu_custom_call" | custom-call | flops 4831838208 | bytes 12582912 | tf_op jit(solution)/shard_map/weight_grad_pair/pallas_call | solution.py:239
  275.2 3.7 all-to-all-start.5
  279.5 17.6 %all-to-all-done.5.dot_t = bf16[4,192,512]{2,1,0:T(8,128)(2,1)S(1)} async-done(((bf16[4,192,512]{2,1,0:T(8,128)(2,1)}), bf16[4,192,512]{2,1,0:T(8,128)(2,1)S(1)}, u32[]{:S(2)}, u32[]{:S(2)}) %all-to-all-start.5) | async-done | bytes 786464 | tf_op jit(solution)/shard_map/all_to_all | solution.py:360
  298.0 41.5 %attend_backward.3 = (bf16[192,1024]{1,0:T(8,128)(2,1)}, bf16[2,384,1024]{2,1,0:T(8,128)(2,1)}, bf16[2,384,1024]{2,1,0:T(8,128)(2,1)}) custom-call(s32[33]{0:T(128)} %get-tuple-element.57.meta, bf16[192,1024]{1,0:T(8,128)(2,1)} %fusion.15.qt, bf16[4,192,256]{2,1,0:T(8,128)(2,1)} %pad_maximum_fusion.8.ot, bf16[4,192,512]{2,1,0:T(8,128)(2,1)} %copy-done.2, ...), custom_call_target="tpu_custom_call" | custom-call | flops 196608 | bytes 196608 | tf_op jit(solution)/shard_map/attend_backward/pallas_call | solution.py:195
  342.8 15.8 %collective-permute-done.9 = bf16[768,384]{1,0:T(8,128)(2,1)S(1)} collective-permute-done((bf16[768,384]{1,0:T(8,128)(2,1)}, bf16[768,384]{1,0:T(8,128)(2,1)S(1)}, u32[]{:S(2)}, u32[]{:S(2)}) %collective-permute-start.9) | collective-permute-done | bytes 589856 | tf_op jit(solution)/shard_map/ppermute | solution.py:258
  359.6 4.2 all-to-all-start.6
  363.9 2.6 add_convert_fusion
  368.0 2.0 collective-permute-start.11
  370.0 21.2 %attend_backward.4 = (bf16[128,1024]{1,0:T(8,128)(2,1)}, bf16[2,256,1024]{2,1,0:T(8,128)(2,1)}, bf16[2,256,1024]{2,1,0:T(8,128)(2,1)}) custom-call(s32[33]{0:T(128)} %get-tuple-element.66.meta, bf16[192,1024]{1,0:T(8,128)(2,1)} %fusion.14.qt, bf16[4,192,256]{2,1,0:T(8,128)(2,1)} %get-tuple-element.55.ot, bf16[4,192,512]{2,1,0:T(8,128)(2,1)} %copy-done.2, ...), custom_call_target="tpu_custom_call" | custom-call | flops 131072 | bytes 131072 | tf_op jit(solution)/shard_map/attend_backward/pallas_call | solution.py:195
  391.3 2.4 collective-permute-start.12
  393.7 4.1 collective-permute-done.12
  401.5 2.6 convolution_convert_fusion.1
  404.2 1.9 add_convert_fusion.1
  407.0 12.2 %attend_backward.5 = (bf16[64,1024]{1,0:T(8,128)(2,1)}, bf16[2,128,1024]{2,1,0:T(8,128)(2,1)}, bf16[2,128,1024]{2,1,0:T(8,128)(2,1)}) custom-call(s32[33]{0:T(128)} %get-tuple-element.66.meta, bf16[192,1024]{1,0:T(8,128)(2,1)} %fusion.14.qt, bf16[4,192,256]{2,1,0:T(8,128)(2,1)} %get-tuple-element.55.ot, bf16[4,192,512]{2,1,0:T(8,128)(2,1)} %copy-done.2, ...), custom_call_target="tpu_custom_call" | custom-call | flops 65536 | bytes 65536 | tf_op jit(solution)/shard_map/attend_backward/pallas_call | solution.py:195
  424.6 9.8 %collective-permute-done.13 = bf16[256,1024]{1,0:T(8,128)(2,1)S(1)} collective-permute-done((bf16[256,1024]{1,0:T(8,128)(2,1)}, bf16[256,1024]{1,0:T(8,128)(2,1)S(1)}, u32[]{:S(2)}, u32[]{:S(2)}) %collective-permute-start.13) | collective-permute-done | bytes 524320 | tf_op jit(solution)/shard_map/ppermute | solution.py:258
  434.5 5.0 collective-permute-done.15
  439.6 2.6 fusion.28
  445.2 2.7 convolution_convert_fusion
  450.9 2.2 collective-permute-done.23
  465.7 3.2 all-to-all-start.7
  475.5 5.3 %collective-permute-done.18 = bf16[576,384]{1,0:T(8,128)(2,1)S(1)} collective-permute-done((bf16[576,384]{1,0:T(8,128)(2,1)S(1)}, bf16[576,384]{1,0:T(8,128)(2,1)S(1)}, u32[]{:S(2)}, u32[]{:S(2)}) %collective-permute-start.18) | collective-permute-done | bytes 442400 | tf_op jit(solution)/shard_map/ppermute | solution.py:258
  484.5 5.3 %collective-permute-done.29 = bf16[384,384]{1,0:T(8,128)(2,1)S(1)} collective-permute-done((bf16[384,384]{1,0:T(8,128)(2,1)S(1)}, bf16[384,384]{1,0:T(8,128)(2,1)S(1)}, u32[]{:S(2)}, u32[]{:S(2)}) %collective-permute-start.29) | collective-permute-done | bytes 294944 | tf_op jit(solution)/shard_map/ppermute | solution.py:258
  (290 shorter events, 80.9 us)
Async XLA Ops:
  10.5 43.4 %all-to-all-start = ((bf16[4,256,768]{2,1,0:T(8,128)(2,1)}), bf16[4,256,768]{2,1,0:T(8,128)(2,1)S(1)}, u32[]{:S(2)}, u32[]{:S(2)}) async-start(bf16[4,256,768]{2,1,0:T(8,128)(2,1)} %broadcast_in_dim.30), calls=%async_computation | async-start | bytes 3145728 | tf_op jit(solution)/shard_map/all_to_all | solution.py:360
  16.9 220.8 %all-gather.2.cloned.1.call-start = ((), (), s32[]{:S(2)}) async-start(), calls=%async_computation.11 | async-start | bytes 10027008 | tf_op jit(solution)/shard_map/all_gather | solution.py:401
  21.6 21.4 %collective-permute-start = (bf16[1152,384]{1,0:T(8,128)(2,1)}, bf16[1152,384]{1,0:T(8,128)(2,1)}, u32[]{:S(2)}, u32[]{:S(2)}) collective-permute-start(bf16[1152,384]{1,0:T(8,128)(2,1)} %constant_dynamic-update-slice_fusion), channel_id=1, source_target_pairs={{0,16},{16,0},{1,17},{17,1},{2,18},{18,2},{3,19},{19,3},{4,20},{20... | collective-permute-start | bytes 2654216 | tf_op jit(solution)/shard_map/ppermute | solution.py:258
  45.5 112.0 %copy-start.4 = (bf16[1152,768]{1,0:T(8,128)(2,1)}, bf16[1152,768]{1,0:T(8,128)(2,1)S(1)}, u32[]{:S(2)}) copy-start(bf16[1152,768]{1,0:T(8,128)(2,1)S(1)} %maximum_select_fusion) | copy-start | bytes 5308420
  53.9 30.9 %copy-start.9 = (bf16[4,256,768]{2,1,0:T(8,128)(2,1)}, bf16[4,256,768]{2,1,0:T(8,128)(2,1)S(1)}, u32[]{:S(2)}) copy-start(bf16[4,256,768]{2,1,0:T(8,128)(2,1)S(1)} %all-to-all-done) | copy-start | bytes 4718596
  55.8 25.1 %collective-permute-start.1 = (bf16[384,1024]{1,0:T(8,128)(2,1)}, bf16[384,1024]{1,0:T(8,128)(2,1)}, u32[]{:S(2)}, u32[]{:S(2)}) collective-permute-start(bf16[384,1024]{1,0:T(8,128)(2,1)} %add_convert_fusion.6.refs_0_), channel_id=1, source_target_pairs={{0,8},{4,12},{8,0},{12,4},{1,9},{5,13},{9,1},{13,5},{2,10},{6,14},... | collective-permute-start | bytes 2359304 | tf_op jit(solution)/shard_map/ppermute | solution.py:258
  58.6 59.7 %all-to-all-start.1 = ((bf16[4,256,768]{2,1,0:T(8,128)(2,1)}), bf16[4,256,768]{2,1,0:T(8,128)(2,1)}, u32[]{:S(2)}, u32[]{:S(2)}) async-start(bf16[4,256,768]{2,1,0:T(8,128)(2,1)} %broadcast_in_dim.31), calls=%async_computation.1 | async-start | bytes 3145728 | tf_op jit(solution)/shard_map/all_to_all | solution.py:360
  63.1 23.1 %collective-permute-start.2 = (bf16[384,1024]{1,0:T(8,128)(2,1)}, bf16[384,1024]{1,0:T(8,128)(2,1)}, u32[]{:S(2)}, u32[]{:S(2)}) collective-permute-start(bf16[384,1024]{1,0:T(8,128)(2,1)} %add_convert_fusion.6.refs_0_), channel_id=1, source_target_pairs={{0,4},{4,0},{8,12},{12,8},{1,5},{5,1},{9,13},{13,9},{2,6},{6,2},{1... | collective-permute-start | bytes 2359304 | tf_op jit(solution)/shard_map/ppermute | solution.py:258
  80.9 5.3 %collective-permute-start.3 = (bf16[384,1024]{1,0:T(8,128)(2,1)}, bf16[384,1024]{1,0:T(8,128)(2,1)}, u32[]{:S(2)}, u32[]{:S(2)}) collective-permute-start(bf16[384,1024]{1,0:T(8,128)(2,1)} %collective-permute-done.1.refs_1_), channel_id=1, source_target_pairs={{0,4},{4,0},{8,12},{12,8},{1,5},{5,1},{9,13},{13,9},{2,6},{6,2},{1... | collective-permute-start | bytes 2359304 | tf_op jit(solution)/shard_map/ppermute | solution.py:258
  120.5 37.0 %collective-permute-start.4 = (bf16[384,1024]{1,0:T(8,128)(2,1)S(1)}, bf16[384,1024]{1,0:T(8,128)(2,1)}, u32[]{:S(2)}, u32[]{:S(2)}) collective-permute-start(bf16[384,1024]{1,0:T(8,128)(2,1)S(1)} %add_convert_fusion.5.refs_0_), channel_id=1, source_target_pairs={{0,8},{4,12},{8,0},{12,4},{1,9},{5,13},{9,1},{13,5},{2,10},{6,14},... | collective-permute-start | bytes 2359304 | tf_op jit(solution)/shard_map/ppermute | solution.py:258
  123.9 33.5 %copy-start.47 = (f32[768]{0:T(1024)S(1)}, f32[768]{0:T(1024)}, u32[]{:S(2)}) copy-start(f32[768]{0:T(1024)} %param.31) | copy-start | bytes 9220
  135.0 27.6 %collective-permute-start.5 = (bf16[384,1024]{1,0:T(8,128)(2,1)S(1)}, bf16[384,1024]{1,0:T(8,128)(2,1)}, u32[]{:S(2)}, u32[]{:S(2)}) collective-permute-start(bf16[384,1024]{1,0:T(8,128)(2,1)S(1)} %add_convert_fusion.5.refs_0_), channel_id=1, source_target_pairs={{0,4},{4,0},{8,12},{12,8},{1,5},{5,1},{9,13},{13,9},{2,6},{6,2},{1... | collective-permute-start | bytes 2359304 | tf_op jit(solution)/shard_map/ppermute | solution.py:258
  157.4 5.1 %collective-permute-start.6 = (bf16[384,1024]{1,0:T(8,128)(2,1)}, bf16[384,1024]{1,0:T(8,128)(2,1)}, u32[]{:S(2)}, u32[]{:S(2)}) collective-permute-start(bf16[384,1024]{1,0:T(8,128)(2,1)} %collective-permute-done.4.refs_1_), channel_id=1, source_target_pairs={{0,4},{4,0},{8,12},{12,8},{1,5},{5,1},{9,13},{13,9},{2,6},{6,2},{1... | collective-permute-start | bytes 2359304 | tf_op jit(solution)/shard_map/ppermute | solution.py:258
  159.0 44.0 %all-to-all-start.2 = ((bf16[4,208,768]{2,1,0:T(8,128)(2,1)}), bf16[4,208,768]{2,1,0:T(8,128)(2,1)S(1)}, u32[]{:S(2)}, u32[]{:S(2)}) async-start(bf16[4,208,768]{2,1,0:T(8,128)(2,1)} %broadcast_in_dim.37), calls=%async_computation.2 | async-start | bytes 2555904 | tf_op jit(solution)/shard_map/all_to_all | solution.py:360
  162.6 44.5 %copy-start.3 = (bf16[2,256,768]{2,1,0:T(8,128)(2,1)S(1)}, bf16[2,256,768]{2,1,0:T(8,128)(2,1)}, u32[]{:S(2)}) copy-start(bf16[2,256,768]{2,1,0:T(8,128)(2,1)} %param.19) | copy-start | bytes 2359300
  162.6 44.5 %copy-start.29 = (f32[768]{0:T(1024)S(1)}, f32[768]{0:T(1024)}, u32[]{:S(2)}) copy-start(f32[768]{0:T(1024)} %param.34) | copy-start | bytes 9220
  203.0 15.6 %all-to-all-start.4 = ((bf16[4,192,256]{2,1,0:T(8,128)(2,1)}), bf16[4,192,256]{2,1,0:T(8,128)(2,1)S(1)}, u32[]{:S(2)}, u32[]{:S(2)}) async-start(bf16[4,192,256]{2,1,0:T(8,128)(2,1)} %get-tuple-element.55.ot), calls=%async_computation.4 | async-start | bytes 786432 | tf_op jit(solution)/shard_map/all_to_all | solution.py:360
  218.6 15.5 %all-to-all-start.3 = ((bf16[4,192,256]{2,1,0:T(8,128)(2,1)}), bf16[4,192,256]{2,1,0:T(8,128)(2,1)}, u32[]{:S(2)}, u32[]{:S(2)}) async-start(bf16[4,192,256]{2,1,0:T(8,128)(2,1)} %pad_maximum_fusion.8.ot), calls=%async_computation.3 | async-start | bytes 786432 | tf_op jit(solution)/shard_map/all_to_all | solution.py:360
  222.7 247.4 %reduce-scatter.8.cloned.1.call-start = ((), (), s32[]{:S(2)}) async-start(), calls=%async_computation.14 | async-start | bytes 10027008 | tf_op jit(solution)/shard_map/reduce_scatter | solution.py:523
  275.2 21.9 %all-to-all-start.5 = ((bf16[4,192,512]{2,1,0:T(8,128)(2,1)}), bf16[4,192,512]{2,1,0:T(8,128)(2,1)S(1)}, u32[]{:S(2)}, u32[]{:S(2)}) async-start(bf16[4,192,512]{2,1,0:T(8,128)(2,1)} %bitcast.26), calls=%async_computation.5 | async-start | bytes 1572864 | tf_op jit(solution)/shard_map/all_to_all | solution.py:360
  339.6 24.3 %collective-permute-start.7 = (bf16[2,384,1024]{2,1,0:T(8,128)(2,1)}, bf16[2,384,1024]{2,1,0:T(8,128)(2,1)}, u32[]{:S(2)}, u32[]{:S(2)}) collective-permute-start(bf16[2,384,1024]{2,1,0:T(8,128)(2,1)} %get-tuple-element.60), channel_id=1, source_target_pairs={{0,4},{4,0},{8,12},{12,8},{1,5},{5,1},{9,13},{13,9},{2,6},{6,2},{1... | collective-permute-start | bytes 4718600 | tf_op jit(solution)/shard_map/ppermute | solution.py:258
  342.7 15.9 %collective-permute-start.9 = (bf16[768,384]{1,0:T(8,128)(2,1)}, bf16[768,384]{1,0:T(8,128)(2,1)S(1)}, u32[]{:S(2)}, u32[]{:S(2)}) collective-permute-start(bf16[768,384]{1,0:T(8,128)(2,1)} %slice.245), channel_id=1, source_target_pairs={{0,16},{16,0},{1,17},{17,1},{2,18},{18,2},{3,19},{19,3},{4,20},{20... | collective-permute-start | bytes 1769480 | tf_op jit(solution)/shard_map/ppermute | solution.py:258
  359.6 38.2 %all-to-all-start.6 = ((bf16[4,192,384]{2,1,0:T(8,128)(2,1)}), bf16[4,192,384]{2,1,0:T(8,128)(2,1)}, u32[]{:S(2)}, u32[]{:S(2)}) async-start(bf16[4,192,384]{2,1,0:T(8,128)(2,1)} %bitcast.32), calls=%async_computation.7 | async-start | bytes 1179648 | tf_op jit(solution)/shard_map/all_to_all | solution.py:360
  363.8 126.0 %reduce-scatter.4.cloned.1.call-start = ((), (), s32[]{:S(2)}) async-start(), calls=%async_computation.12 | async-start | bytes 1966080 | tf_op jit(solution)/shard_map/reduce_scatter | solution.py:570
  367.5 31.7 %collective-permute-start.8 = (bf16[384,1024]{1,0:T(8,128)(2,1)}, bf16[384,1024]{1,0:T(8,128)(2,1)}, u32[]{:S(2)}, u32[]{:S(2)}) collective-permute-start(bf16[384,1024]{1,0:T(8,128)(2,1)} %slice_bitcast_fusion.10), channel_id=1, source_target_pairs={{0,8},{4,12},{8,0},{12,4},{1,9},{5,13},{9,1},{13,5},{2,10},{6,14},... | collective-permute-start | bytes 2359304 | tf_op jit(solution)/shard_map/ppermute | solution.py:258
  368.0 23.2 %collective-permute-start.11 = (f32[8448]{0:T(1024)S(1)}, f32[8448]{0:T(1024)S(1)}, u32[]{:S(2)}, u32[]{:S(2)}) collective-permute-start(f32[8448]{0:T(1024)S(1)} %pad_add_fusion), channel_id=1, source_target_pairs={{0,1},{1,0},{2,3},{3,2},{4,5},{5,4},{6,7},{7,6},{8,9},{9,8},{10,11... | collective-permute-start | bytes 101384 | tf_op jit(solution)/shard_map/ppermute | solution.py:258
  391.3 13.0 %collective-permute-start.10 = (bf16[2,256,1024]{2,1,0:T(8,128)(2,1)}, bf16[2,256,1024]{2,1,0:T(8,128)(2,1)}, u32[]{:S(2)}, u32[]{:S(2)}) collective-permute-start(bf16[2,256,1024]{2,1,0:T(8,128)(2,1)} %get-tuple-element.65), channel_id=1, source_target_pairs={{0,4},{4,0},{8,12},{12,8},{1,5},{5,1},{9,13},{13,9},{2,6},{6,2},{1... | collective-permute-start | bytes 3145736 | tf_op jit(solution)/shard_map/ppermute | solution.py:258
  391.3 6.6 %collective-permute-start.12 = (f32[8448]{0:T(1024)S(1)}, f32[8448]{0:T(1024)S(1)}, u32[]{:S(2)}, u32[]{:S(2)}) collective-permute-start(f32[8448]{0:T(1024)S(1)} %fusion.61), channel_id=1, source_target_pairs={{0,2},{1,3},{2,0},{3,1},{4,6},{5,7},{6,4},{7,5},{8,10},{9,11},{10,... | collective-permute-start | bytes 101384 | tf_op jit(solution)/shard_map/ppermute | solution.py:258
  404.2 85.6 %reduce-scatter.6.cloned.1.call-start = ((), (), s32[]{:S(2)}) async-start(), calls=%async_computation.13 | async-start | bytes 1966080 | tf_op jit(solution)/shard_map/reduce_scatter | solution.py:570
  419.2 2.1 collective-permute-start.14
  419.4 14.9 %collective-permute-start.13 = (bf16[256,1024]{1,0:T(8,128)(2,1)}, bf16[256,1024]{1,0:T(8,128)(2,1)S(1)}, u32[]{:S(2)}, u32[]{:S(2)}) collective-permute-start(bf16[256,1024]{1,0:T(8,128)(2,1)} %slice_bitcast_fusion.12), channel_id=1, source_target_pairs={{0,8},{4,12},{8,0},{12,4},{1,9},{5,13},{9,1},{13,5},{2,10},{6,14},... | collective-permute-start | bytes 1572872 | tf_op jit(solution)/shard_map/ppermute | solution.py:258
  422.6 16.9 %collective-permute-start.15 = (bf16[128,1024]{1,0:T(8,128)(2,1)S(1)}, bf16[128,1024]{1,0:T(8,128)(2,1)S(1)}, u32[]{:S(2)}, u32[]{:S(2)}) collective-permute-start(bf16[128,1024]{1,0:T(8,128)(2,1)S(1)} %slice_bitcast_fusion.17), channel_id=1, source_target_pairs={{0,8},{4,12},{8,0},{12,4},{1,9},{5,13},{9,1},{13,5},{2,10},{6,14},... | collective-permute-start | bytes 786440 | tf_op jit(solution)/shard_map/ppermute | solution.py:258
  444.6 14.4 %collective-permute-start.16 = (bf16[576,384]{1,0:T(8,128)(2,1)}, bf16[576,384]{1,0:T(8,128)(2,1)}, u32[]{:S(2)}, u32[]{:S(2)}) collective-permute-start(bf16[576,384]{1,0:T(8,128)(2,1)} %slice.253), channel_id=1, source_target_pairs={{0,16},{16,0},{1,17},{17,1},{2,18},{18,2},{3,19},{19,3},{4,20},{20... | collective-permute-start | bytes 1327112 | tf_op jit(solution)/shard_map/ppermute | solution.py:258
  447.9 1.3 collective-permute-start.22
  449.2 4.0 collective-permute-start.23
  453.1 4.2 collective-permute-start.24
  455.8 1.6 collective-permute-start.19
  457.3 5.7 %collective-permute-start.25 = (bf16[192,384]{1,0:T(8,128)(2,1)S(1)}, bf16[192,384]{1,0:T(8,128)(2,1)S(1)}, u32[]{:S(2)}, u32[]{:S(2)}) collective-permute-start(bf16[192,384]{1,0:T(8,128)(2,1)S(1)} %convert_reduce_fusion.4), channel_id=1, source_target_pairs={{0,4},{4,0},{8,12},{12,8},{1,5},{5,1},{9,13},{13,9},{2,6},{6,2},{1... | collective-permute-start | bytes 442376 | tf_op jit(solution)/shard_map/ppermute | solution.py:258
  457.3 4.2 collective-permute-start.20
  460.1 8.9 %collective-permute-start.17 = (bf16[576,384]{1,0:T(8,128)(2,1)S(1)}, bf16[576,384]{1,0:T(8,128)(2,1)S(1)}, u32[]{:S(2)}, u32[]{:S(2)}) collective-permute-start(bf16[576,384]{1,0:T(8,128)(2,1)S(1)} %add_convert_fusion.11), channel_id=1, source_target_pairs={{0,4},{4,0},{8,12},{12,8},{1,5},{5,1},{9,13},{13,9},{2,6},{6,2},{1... | collective-permute-start | bytes 1327112 | tf_op jit(solution)/shard_map/ppermute | solution.py:258
  461.6 3.6 collective-permute-start.21
  463.7 9.4 %collective-permute-start.26 = (bf16[192,384]{1,0:T(8,128)(2,1)}, bf16[192,384]{1,0:T(8,128)(2,1)S(1)}, u32[]{:S(2)}, u32[]{:S(2)}) collective-permute-start(bf16[192,384]{1,0:T(8,128)(2,1)} %add_convert_fusion.13), channel_id=1, source_target_pairs={{0,8},{4,12},{8,0},{12,4},{1,9},{5,13},{9,1},{13,5},{2,10},{6,14},... | collective-permute-start | bytes 442376 | tf_op jit(solution)/shard_map/ppermute | solution.py:258
  465.7 9.1 %all-to-all-start.7 = ((f32[4,1,192]{2,1,0:T(1,128)}), f32[4,1,192]{2,1,0:T(1,128)S(1)}, u32[]{:S(2)}, u32[]{:S(2)}) async-start(f32[4,1,192]{2,1,0:T(1,128)} %broadcast_in_dim.43), calls=%async_computation.9 | async-start | bytes 8192 | tf_op jit(solution)/shard_map/all_to_all | solution.py:360
  469.1 11.7 %collective-permute-start.18 = (bf16[576,384]{1,0:T(8,128)(2,1)S(1)}, bf16[576,384]{1,0:T(8,128)(2,1)S(1)}, u32[]{:S(2)}, u32[]{:S(2)}) collective-permute-start(bf16[576,384]{1,0:T(8,128)(2,1)S(1)} %add_convert_fusion.10), channel_id=1, source_target_pairs={{0,8},{4,12},{8,0},{12,4},{1,9},{5,13},{9,1},{13,5},{2,10},{6,14},... | collective-permute-start | bytes 1327112 | tf_op jit(solution)/shard_map/ppermute | solution.py:258
  471.6 9.3 %collective-permute-start.27 = (bf16[384,384]{1,0:T(8,128)(2,1)S(1)}, bf16[384,384]{1,0:T(8,128)(2,1)}, u32[]{:S(2)}, u32[]{:S(2)}) collective-permute-start(bf16[384,384]{1,0:T(8,128)(2,1)S(1)} %slice.265), channel_id=1, source_target_pairs={{0,16},{16,0},{1,17},{17,1},{2,18},{18,2},{3,19},{19,3},{4,20},{20... | collective-permute-start | bytes 884744 | tf_op jit(solution)/shard_map/ppermute | solution.py:258
  482.0 7.8 %collective-permute-start.29 = (bf16[384,384]{1,0:T(8,128)(2,1)S(1)}, bf16[384,384]{1,0:T(8,128)(2,1)S(1)}, u32[]{:S(2)}, u32[]{:S(2)}) collective-permute-start(bf16[384,384]{1,0:T(8,128)(2,1)S(1)} %add_convert_fusion.12), channel_id=1, source_target_pairs={{0,8},{4,12},{8,0},{12,4},{1,9},{5,13},{9,1},{13,5},{2,10},{6,14},... | collective-permute-start | bytes 884744 | tf_op jit(solution)/shard_map/ppermute | solution.py:258
  484.5 7.6 %collective-permute-start.28 = (bf16[384,384]{1,0:T(8,128)(2,1)S(1)}, bf16[384,384]{1,0:T(8,128)(2,1)S(1)}, u32[]{:S(2)}, u32[]{:S(2)}) collective-permute-start(bf16[384,384]{1,0:T(8,128)(2,1)S(1)} %add_convert_fusion.12), channel_id=1, source_target_pairs={{0,4},{4,0},{8,12},{12,8},{1,5},{5,1},{9,13},{13,9},{2,6},{6,2},{1... | collective-permute-start | bytes 884744 | tf_op jit(solution)/shard_map/ppermute | solution.py:258
  489.8 2.2 collective-permute-start.30
  (52 other events, 342.8 us)
Sparse Core Ops, SparseCore 0:
  54.0 135.3 all-gather.1
  275.3 124.3 reduce-scatter.7
  404.3 34.0 reduce-scatter.3
  448.0 34.8 reduce-scatter.5
